TPU v7x, 128 devices: a whole 4x4x4 slice. The times are simulated.
128 devices in a mesh: gx: 16 (over z, y_lo, core), gy: 8 (over x, y_hi).
Axes of the slice: x: 4, y: 4 (y_hi: 2, y_lo: 2; y = y_hi * 2 + y_lo), z: 4, core: 2. Of those that a mesh axis runs over, the one named last changes fastest.
Arguments:
- mean_field: float32 [256, 512, 128], P('gx', 'gy'), may hold values from -3 to 3
- log_scale: float32 [256, 512, 128], P('gx', 'gy'), may hold values from -2.5 to -0.7
- noise: float32 [256, 512, 128], P('gx', 'gy'), may hold values from -6 to 6
- wave_prev: float32 [256, 512, 128], P('gx', 'gy'), may hold values from -6 to 6
- wave_now: float32 [256, 512, 128], P('gx', 'gy'), may hold values from -6 to 6
- adjoint_next: float32 [256, 512, 128], P('gx', 'gy'), may hold values from -6 to 6
- adjoint_now: float32 [256, 512, 128], P('gx', 'gy'), may hold values from -6 to 6
- sources: int32 [16, 3], replicated, may hold values from 0 to 511, as said below
- receivers: int32 [256, 3], replicated, may hold values from 0 to 511, as said below
- observed: float32 [256], replicated, may hold values from -6 to 6
- step_index: int32 [1], replicated, may hold values from 0 to 47
- prior_scale: float32 [1], replicated, may hold values from 0.5 to 2
Outputs:
- wave_next: float32 [256, 512, 128], P('gx', 'gy')
- adjoint_prev: float32 [256, 512, 128], P('gx', 'gy')
- search: float32 [256, 512, 128], P('gx', 'gy')
- logscale_grad: float32 [256, 512, 128], P('gx', 'gy')
Inputs may be any that keep to these rules, and one draw needn't show every extreme that they name: `sources`: each row gives the first, second and depth cell of a point, below 256, 512 and 128; points may coincide. `receivers`: each row gives the first, second and depth cell of a point, below 256, 512 and 128; points may coincide.
All inputs are finite; a program needn't handle non-finite values.
Results may differ from a plain program's by a relative error of at most 0.000075.
Values sent between devices are 32-bit elements; how exact they have to be, the bound alone decides.
No kernel may reach another device: no remote copies, remote signals or barrier semaphores. Data moves between devices by JAX's collectives and lax.ppermute only.
A program may use at most 64 MiB of HBM per device.

v0:
```python
import functools
import math

import jax
import jax.numpy as jnp
import numpy as np
from jax import lax
from jax.experimental import pallas as pl
from jax.experimental.pallas import tpu as pltpu
from jax.sharding import PartitionSpec as P

NSTEPS = 48
STENCIL_WEIGHTS = (-205.0 / 72.0, 8.0 / 5.0, -1.0 / 5.0, 8.0 / 315.0, -1.0 / 560.0)
COURANT_SQUARED = 0.08
VELOCITY_GAIN = 0.2
PULSE_FREQUENCY = 0.05
PULSE_AMPLITUDE = 20.0

F32 = jnp.float32
BF16 = jnp.bfloat16
ROW = (((1,), (0,)), ((), ()))
TRANSPOSED_RIGHT = (((1,), (1,)), ((), ()))
TRANSPOSED_LEFT = (((0,), (0,)), ((), ()))


def hartley(length):
    index = np.arange(length)
    angle = (index[:, None] * index[None, :] % length) * (2.0 * np.pi / length)
    return np.cos(angle) + np.sin(angle)


def halves(matrix):
    high = matrix.astype(np.float32).astype(jnp.bfloat16)
    low = (matrix - high.astype(np.float64)).astype(np.float32).astype(jnp.bfloat16)
    return np.stack([high, low])


def wave_terms(length):
    return (length / 8.0) ** 2 * 4.0 * np.sin(np.arange(length) * (np.pi / length)) ** 2


def band(length):
    matrix = np.zeros((length, length))
    for offset in range(5):
        weight = STENCIL_WEIGHTS[offset] * (3.0 if offset == 0 else 1.0)
        matrix += weight * np.eye(length, k=offset)
        if offset:
            matrix += weight * np.eye(length, k=-offset)
    return matrix


def split(value):
    high = value.astype(BF16)
    return high, (value - high.astype(F32)).astype(BF16)


def dot(left, right, dims=ROW):
    return lax.dot_general(left, right, dims, preferred_element_type=F32)


def dot_3(left, right, dims=ROW):
    total = dot(left[0], right[1], dims) + dot(left[1], right[0], dims)
    return total + dot(left[0], right[0], dims)


def edges_kernel(mean, logs, noise, adjoint, wave, xlow, xhigh, ylow, yhigh):
    nx, ny, _ = wave.shape

    def scaled(a, b, c, d):
        where = (slice(a, b), slice(c, d))
        sample = mean[where] + jnp.exp(logs[where]) * noise[where]
        return COURANT_SQUARED * jnp.exp(2.0 * VELOCITY_GAIN * sample) * adjoint[where]

    xlow[0] = wave[0:4]
    xhigh[0] = wave[nx - 4 : nx]
    xlow[1] = scaled(0, 4, 0, ny)
    xhigh[1] = scaled(nx - 4, nx, 0, ny)
    for start in range(0, nx, 4):
        if start == 0:
            low, high = xlow[1, :, 0:8], xhigh[1, :, 0:8]
        for kind in range(2):
            if kind == 0:
                first, last = wave[start : start + 4, 0:8], wave[start : start + 4, ny - 8 : ny]
            elif start == 0:
                first, last = xlow[1, :, 0:8], xlow[1, :, ny - 8 : ny]
            elif start == nx - 4:
                first, last = xhigh[1, :, 0:8], xhigh[1, :, ny - 8 : ny]
            else:
                first = scaled(start, start + 4, 0, 8)
                last = scaled(start, start + 4, ny - 8, ny)
            for pair in range(2):
                at = start // 2 + pair
                ylow[kind, at] = jnp.concatenate([first[2 * pair, 0:4], first[2 * pair + 1, 0:4]], 0)
                yhigh[kind, at] = jnp.concatenate([last[2 * pair, 4:8], last[2 * pair + 1, 4:8]], 0)


def local_kernel(
    codes, mean, logs, noise, wave, wave_prev, adjoint, adjoint_next, bands,
    curved, base_wave, base_adjoint, speed, tilt, sample, listed,
    field, plane,
):
    nx, ny, nz = wave.shape
    points = codes.shape[0]
    sources = 16

    def scan(start, stop, at):
        def step(i, count):
            code = codes[i]
            listed[at + count] = i
            return count + (code >= 0).astype(jnp.int32)

        return lax.fori_loop(start, stop, step, jnp.int32(0), unroll=8)

    n_sources = scan(0, sources, 0)
    n_receivers = scan(sources, points, sources + 1)
    listed[points + 2] = n_sources
    listed[points + 3] = n_receivers

    for kind in range(2):
        field[kind, 0:4] = jnp.zeros((4, ny + 16, nz), F32)
        field[kind, nx + 4 : nx + 8] = jnp.zeros((4, ny + 16, nz), F32)
        field[kind, :, 0:8] = jnp.zeros((nx + 8, 8, nz), F32)
        field[kind, :, ny + 8 : ny + 16] = jnp.zeros((nx + 8, 8, nz), F32)

    def prepare(x, _):
        spread_noise = jnp.exp(logs[x]) * noise[x]
        value = mean[x] + spread_noise
        rate = COURANT_SQUARED * jnp.exp(2.0 * VELOCITY_GAIN * value)
        tilt[x] = spread_noise
        sample[x] = value
        speed[x] = rate
        field[0, x + 4, 8 : ny + 8] = wave[x]
        field[1, x + 4, 8 : ny + 8] = rate * adjoint[x]
        return 0

    lax.fori_loop(0, nx, prepare, 0)

    for kind in range(2):
        value = field[kind, 4 : nx + 4, 8 : ny + 8].reshape(nx * ny, nz)
        plane[kind] = lax.dot_general(
            value, bands[...], ROW, precision=lax.Precision.HIGHEST, preferred_element_type=F32
        )

    def lateral(kind, x):
        total = plane[kind, pl.ds(pl.multiple_of(x * ny, ny), ny)]
        for offset in range(1, 5):
            near = field[kind, x + 4 + offset, 8 : ny + 8] + field[kind, x + 4 - offset, 8 : ny + 8]
            near = near + field[kind, x + 4, 8 + offset : ny + 8 + offset]
            near = near + field[kind, x + 4, 8 - offset : ny + 8 - offset]
            total = total + STENCIL_WEIGHTS[offset] * near
        return total

    def finish(x, _):
        bend = lateral(0, x)
        curved[x] = bend
        base_wave[x] = 2.0 * wave[x] - wave_prev[x] + speed[x] * bend
        base_adjoint[x] = 2.0 * adjoint[x] - adjoint_next[x] + lateral(1, x)
        return 0

    lax.fori_loop(0, nx, finish, 0)


def finish_kernel(
    codes, listed, observed, scalars, curved, base_wave, base_adjoint, speed, tilt,
    xlow, xhigh, ylow, yhigh, forward_z,
    wave_next, adjoint_prev, logscale_grad, spectra,
    slope,
):
    nx, ny, nz = curved.shape
    points = codes.shape[0]
    sources = 16
    row_at = lax.broadcasted_iota(jnp.int32, (8, nz), 0)
    lane_at = lax.broadcasted_iota(jnp.int32, (1, nz), 1)
    keep = [scalars[i] for i in range(4)]
    pulse = scalars[4]

    def lateral_y(kind, x):
        start = jnp.zeros((8, nz), F32)
        end = jnp.zeros((8, nz), F32)
        low, high = ylow[kind, x // 2], yhigh[kind, x // 2]
        mine = row_at < 4 if x % 2 == 0 else row_at >= 4
        low, high = jnp.where(mine, low, 0.0), jnp.where(mine, high, 0.0)
        base = 0 if x % 2 == 0 else 4
        for offset in range(1, 5):
            start = start + STENCIL_WEIGHTS[offset] * pltpu.roll(low, (offset - 4 - base) % 8, 0)
            end = end + STENCIL_WEIGHTS[offset] * pltpu.roll(high, (8 - offset - base) % 8, 0)
        return jnp.where(row_at < 4, start, 0.0) * keep[2], jnp.where(row_at >= 4, end, 0.0) * keep[3]

    def change(kind, x):
        start, end = lateral_y(kind, x)
        total = jnp.concatenate([start, jnp.zeros((ny - 16, nz), F32), end], 0)
        side = None
        for offset in range(1, 5):
            if x - offset < 0:
                term = STENCIL_WEIGHTS[offset] * keep[0] * xlow[kind, x - offset + 4]
            elif x + offset >= nx:
                term = STENCIL_WEIGHTS[offset] * keep[1] * xhigh[kind, x + offset - nx]
            else:
                continue
            total = total + term
        return total

    for x in range(nx):
        more = change(0, x)
        bend = curved[x] + more
        rows = slice(x * ny, (x + 1) * ny)
        wave_next[rows] = base_wave[x] + speed[x] * more
        adjoint_prev[rows] = base_adjoint[x] + change(1, x)
        slope[rows] = (2.0 * VELOCITY_GAIN) * speed[x] * bend

    def shoot(i, _):
        code = codes[listed[i]]
        row = code // nz
        hit = lane_at == code % nz
        wave_next[pl.ds(row, 1)] = wave_next[pl.ds(row, 1)] + jnp.where(hit, pulse, 0.0)
        return 0

    lax.fori_loop(0, listed[points + 2], shoot, 0)

    def record(i, _):
        point = listed[sources + 1 + i]
        code = codes[point]
        row = code // nz
        hit = lane_at == code % nz
        misfit = wave_next[pl.ds(row, 1)] - observed[point - sources]
        adjoint_prev[pl.ds(row, 1)] = adjoint_prev[pl.ds(row, 1)] + jnp.where(hit, misfit, 0.0)
        return 0

    lax.fori_loop(0, listed[points + 3], record, 0)

    matrix = (forward_z[0], forward_z[1])
    for j in range(nx // 2):
        rows = slice(2 * j * ny, 2 * (j + 1) * ny)
        grad = slope[rows] * adjoint_prev[rows]
        logscale_grad[rows] = grad * tilt[2 * j : 2 * j + 2].reshape(2 * ny, nz) - 1.0
        spectra[pl.ds(j, nz, stride=8)] = dot_3(matrix, split(grad), TRANSPOSED_RIGHT)


def filter_kernel(scalars, spectra, matrix_y, matrix_x, terms_x, terms_y, result, plane):
    half = plane.shape[0] // 2
    tiles_x, tiles_y = spectra.shape[0], spectra.shape[1]
    lane = lax.broadcasted_iota(jnp.int32, (half, 128), 1)
    for m in range(tiles_y // 2):
        even = spectra[:, 2 * m].reshape(half, 128)
        odd = spectra[:, 2 * m + 1].reshape(half, 128)
        columns = slice(128 * m, 128 * (m + 1))
        plane[0:half, columns] = jnp.where(lane < 64, even, pltpu.roll(odd, 64, 1))
        plane[half:, columns] = jnp.where(lane < 64, pltpu.roll(even, 64, 1), odd)
    pair_y = (matrix_y[0], matrix_y[1])
    pair_x = (matrix_x[0], matrix_x[1])
    value = dot_3(split(plane[...]), pair_y)
    value = dot_3(pair_x, split(value))
    value = value * (scalars[0] / ((scalars[1] + terms_x[...]) + terms_y[...]))
    value = dot_3(pair_x, split(value), TRANSPOSED_LEFT)
    plane[...] = dot_3(split(value), pair_y)
    for m in range(tiles_y // 2):
        columns = slice(128 * m, 128 * (m + 1))
        even, odd = plane[0:half, columns], plane[half:, columns]
        first = jnp.where(lane < 64, even, pltpu.roll(odd, 64, 1))
        second = jnp.where(lane < 64, pltpu.roll(even, 64, 1), odd)
        result[:, 2 * m] = first.reshape(tiles_x, 8, 128)
        result[:, 2 * m + 1] = second.reshape(tiles_x, 8, 128)


def back_kernel(spectra, inverse_z, sample, search):
    nx, ny, nz = sample.shape
    matrix = (inverse_z[0], inverse_z[1])
    for j in range(nx // 2):
        value = split(spectra[pl.ds(j, nz, stride=8)])
        smooth = dot_3(value, matrix, TRANSPOSED_LEFT)
        search[2 * j : 2 * j + 2] = smooth.reshape(2, ny, nz) + sample[2 * j : 2 * j + 2]


SMEM = pl.BlockSpec(memory_space=pltpu.SMEM)
VMEM = pl.BlockSpec(memory_space=pltpu.VMEM)


def shape(*sizes):
    return jax.ShapeDtypeStruct(sizes, F32)


def per_device(
    mean_field,
    log_scale,
    noise,
    wave_prev,
    wave_now,
    adjoint_next,
    adjoint_now,
    sources,
    receivers,
    observed,
    step_index,
    prior_scale,
):
    nx, ny, nz = wave_now.shape
    parts_x, parts_y = lax.axis_size("gx"), lax.axis_size("gy")
    index_x, index_y = lax.axis_index("gx"), lax.axis_index("gy")
    total_x, total_y = nx * parts_x, ny * parts_y
    block = shape(nx, ny, nz)
    flat = shape(nx * ny, nz)

    xlow, xhigh, ylow, yhigh = pl.pallas_call(
        edges_kernel,
        out_shape=(shape(2, 4, ny, nz),) * 2 + (shape(2, nx // 2, 8, nz),) * 2,
        in_specs=[VMEM] * 5,
        out_specs=(VMEM,) * 4,
        name="edges",
    )(mean_field, log_scale, noise, adjoint_now, wave_now)

    up_x = [(i, (i + 1) % parts_x) for i in range(parts_x)]
    down_x = [(j, i) for i, j in up_x]
    up_y = [(i, (i + 1) % parts_y) for i in range(parts_y)]
    down_y = [(j, i) for i, j in up_y]
    from_low_x = lax.ppermute(xhigh, "gx", up_x)
    from_high_x = lax.ppermute(xlow, "gx", down_x)
    from_low_y = lax.ppermute(yhigh, "gy", up_y)
    from_high_y = lax.ppermute(ylow, "gy", down_y)

    points = jnp.concatenate([sources, receivers], axis=0)
    at_x = points[:, 0] - index_x * nx
    at_y = points[:, 1] - index_y * ny
    inside = (at_x >= 0) & (at_x < nx) & (at_y >= 0) & (at_y < ny)
    codes = jnp.where(inside, (at_x * ny + at_y) * nz + points[:, 2], -1)
    n_points = points.shape[0]

    moment = (step_index[0] - NSTEPS // 2).astype(F32) * (math.pi * PULSE_FREQUENCY)
    pulse = PULSE_AMPLITUDE * (1.0 - 2.0 * moment * moment) * jnp.exp(-moment * moment)
    scalars = jnp.stack(
        [
            (index_x > 0).astype(F32),
            (index_x < parts_x - 1).astype(F32),
            (index_y > 0).astype(F32),
            (index_y < parts_y - 1).astype(F32),
            pulse,
        ]
    )

    bands = jnp.asarray(band(nz).astype(np.float32))
    curved, base_wave, base_adjoint, speed, tilt, sample, listed = pl.pallas_call(
        local_kernel,
        out_shape=(block,) * 6 + (jax.ShapeDtypeStruct((n_points + 4,), jnp.int32),),
        in_specs=[SMEM] + [VMEM] * 8,
        out_specs=(VMEM,) * 6 + (SMEM,),
        scratch_shapes=[
            pltpu.VMEM((2, nx + 8, ny + 16, nz), F32),
            pltpu.VMEM((2, nx * ny, nz), F32),
        ],
        name="local",
    )(codes, mean_field, log_scale, noise, wave_now, wave_prev, adjoint_now, adjoint_next, bands)

    matrix_z = hartley(nz)
    forward_z = jnp.asarray(halves(matrix_z))
    wave_next, adjoint_prev, logscale_grad, spectra = pl.pallas_call(
        finish_kernel,
        out_shape=(flat,) * 4,
        in_specs=[SMEM] * 4 + [VMEM] * 10,
        out_specs=(VMEM,) * 4,
        scratch_shapes=[pltpu.VMEM((nx * ny, nz), F32)],
        name="finish",
    )(
        codes, listed, observed, scalars, curved, base_wave, base_adjoint, speed, tilt,
        from_low_x, from_high_x, from_low_y, from_high_y, forward_z,
    )

    spectra = lax.all_to_all(
        spectra.reshape(nz, 8, nz), ("gx", "gy"), split_axis=0, concat_axis=0, tiled=True
    )

    order = np.arange(total_x).reshape(parts_x, nx // 2, 2).transpose(2, 0, 1).reshape(-1)
    matrix_x = jnp.asarray(halves(hartley(total_x)[:, order]))
    matrix_y = jnp.asarray(halves(hartley(total_y)))
    terms_x = jnp.asarray(wave_terms(total_x).astype(np.float32)[:, None])
    terms_y = jnp.asarray(wave_terms(total_y).astype(np.float32)[None, :])
    terms_z = jnp.asarray(wave_terms(nz).astype(np.float32))
    depth_term = lax.dynamic_index_in_dim(terms_z, index_x * parts_y + index_y, keepdims=False)
    cells = total_x * total_y * nz
    gain = jnp.stack([prior_scale[0] * (math.sqrt(cells) / 8.0 / cells), 1.0 + depth_term])
    filtered = pl.pallas_call(
        filter_kernel,
        out_shape=shape(parts_x, parts_y, 8, nz),
        in_specs=[SMEM] + [VMEM] * 5,
        out_specs=VMEM,
        scratch_shapes=[pltpu.VMEM((total_x, total_y), F32)],
        name="filter",
    )(gain, spectra.reshape(parts_x, parts_y, 8, nz), matrix_y, matrix_x, terms_x, terms_y)

    filtered = lax.all_to_all(
        filtered.reshape(nz, 8, nz), ("gx", "gy"), split_axis=0, concat_axis=0, tiled=True
    )
    search = pl.pallas_call(
        back_kernel,
        out_shape=block,
        in_specs=[VMEM] * 3,
        out_specs=VMEM,
        name="back",
    )(filtered.reshape(nx * ny, nz), forward_z, sample)
    return (
        wave_next.reshape(nx, ny, nz),
        adjoint_prev.reshape(nx, ny, nz),
        search,
        logscale_grad.reshape(nx, ny, nz),
    )


def solution(mesh):
    grid = P("gx", "gy", None)
    return jax.shard_map(
        per_device,
        mesh=mesh,
        in_specs=(grid,) * 7 + (P(),) * 5,
        out_specs=(grid,) * 4,
        check_vma=False,
    )
```

profile of v0, /device:TPU:1, one launch (start us, length us, event | category | flops | bytes accessed | tf_op | source)
XLA Modules:
  0.0 75.3 jit_solution(86331618911633588)
XLA Ops:
  0.6 2.5 %edges.1 = (f32[2,4,64,128]{3,2,1,0:T(8,128)}, f32[2,4,64,128]{3,2,1,0:T(8,128)}, f32[2,8,8,128]{3,2,1,0:T(8,128)}, f32[2,8,8,128]{3,2,1,0:T(8,128)}) custom-call(f32[16,64,128]{2,1,0:T(8,128)} %mean.3, f32[16,64,128]{2,1,0:T(8,128)} %logs.3, f32[16,64,128]{2,1,0:T(8,128)} %noise.3, f32[16,64,128]{2,1,0:T(8,128)} %adjoint.3, f32[16,64,128]{2,1,0:T(8,128)} %wave.3), custom_call_target="tpu_custom_call" | custom-call | tf_op jit(solution)/shard_map/edges/pallas_call | solution.py:303
  3.2 2.7 %collective-permute-start = (f32[2,4,64,128]{3,2,1,0:T(8,128)}, f32[2,4,64,128]{3,2,1,0:T(8,128)S(1)}, u32[]{:S(2)}, u32[]{:S(2)}) collective-permute-start(f32[2,4,64,128]{3,2,1,0:T(8,128)} %get-tuple-element.25), channel_id=1, source_target_pairs={{0,8},{8,16},{16,24},{24,32},{32,40},{40,48},{48,56},{56,64},{64,7... | collective-permute-start | bytes 786440 | tf_op jit(solution)/shard_map/ppermute | solution.py:315
  5.9 0.0 collective-permute-start.1
  5.9 2.6 %collective-permute-start.2 = (f32[2,8,8,128]{3,2,1,0:T(8,128)}, f32[2,8,8,128]{3,2,1,0:T(8,128)S(1)}, u32[]{:S(2)}, u32[]{:S(2)}) collective-permute-start(f32[2,8,8,128]{3,2,1,0:T(8,128)} %get-tuple-element.27), channel_id=1, source_target_pairs={{0,1},{1,2},{2,3},{3,4},{4,5},{5,6},{6,7},{7,0},{8,9},{9,10},{10,1... | collective-permute-start | bytes 196616 | tf_op jit(solution)/shard_map/ppermute | solution.py:317
  8.5 2.5 %collective-permute-start.3 = (f32[2,8,8,128]{3,2,1,0:T(8,128)}, f32[2,8,8,128]{3,2,1,0:T(8,128)S(1)}, u32[]{:S(2)}, u32[]{:S(2)}) collective-permute-start(f32[2,8,8,128]{3,2,1,0:T(8,128)} %get-tuple-element.28), channel_id=1, source_target_pairs={{1,0},{2,1},{3,2},{4,3},{5,4},{6,5},{7,6},{0,7},{9,8},{10,9},{11,1... | collective-permute-start | bytes 196616 | tf_op jit(solution)/shard_map/ppermute | solution.py:318
  11.6 0.0 copy-start.5
  11.6 0.0 copy-start.6
  11.7 0.7 copy-done.5
  12.3 0.0 copy-done.6
  12.3 0.7 fusion.1.codes
  13.0 7.0 %local.1 = (f32[16,64,128]{2,1,0:T(8,128)}, f32[16,64,128]{2,1,0:T(8,128)}, f32[16,64,128]{2,1,0:T(8,128)}, f32[16,64,128]{2,1,0:T(8,128)}, f32[16,64,128]{2,1,0...) custom-call(s32[272]{0:T(512)} %fusion.1.codes, f32[16,64,128]{2,1,0:T(8,128)} %mean.3, f32[16,64,128]{2,1,0:T(8,128)} %logs.3, ...), custom_call_target="tpu_custom_call" | custom-call | tf_op jit(solution)/shard_map/local/pallas_call | solution.py:340
  20.1 0.6 stack.44.scalars
  20.7 0.0 collective-permute-done.2.ylow
  20.7 0.0 collective-permute-done.3.yhigh
  20.7 0.0 collective-permute-done.xlow
  20.7 0.0 copy-start.1
  20.7 0.0 collective-permute-done.1.xhigh
  20.7 0.6 copy-done.3
  21.3 0.0 copy-done.4
  21.3 0.1 copy-done.1
  21.4 0.1 copy-done.2
  21.5 3.7 %finish.1 = (f32[1024,128]{1,0:T(8,128)}, f32[1024,128]{1,0:T(8,128)}, f32[1024,128]{1,0:T(8,128)}, f32[1024,128]{1,0:T(8,128)}) custom-call(s32[272]{0:T(512)} %fusion.1.codes, s32[276]{0:T(512)} %get-tuple-element.19.listed, f32[256]{0:T(256)} %observed.1, f32[5]{0:T(128)} %stack.44.scalars, f32[16,64,128]{2,1,0:T(8,128)} %get-tuple-element.20.curved, ...), custom_call_target="tpu_custom_call" | custom-call | tf_op jit(solution)/shard_map/finish/pallas_call | solution.py:354
  25.2 9.8 %all-to-all-start = ((f32[128,8,128]{2,1,0:T(8,128)}), f32[128,8,128]{2,1,0:T(8,128)S(1)}, u32[]{:S(2)}, u32[]{:S(2)}) async-start(f32[128,8,128]{2,1,0:T(8,128)} %bitcast.17), calls=%async_computation | async-start | bytes 1048576 | tf_op jit(solution)/shard_map/all_to_all | solution.py:366
  35.7 0.0 copy-start.7
  35.7 0.6 copy-done.7
  36.4 0.6 dynamic_slice.4
  37.6 0.7 pad_maximum_fusion.scalars
  38.3 10.8 %all-to-all-done = f32[128,8,128]{2,1,0:T(8,128)S(1)} async-done(((f32[128,8,128]{2,1,0:T(8,128)}), f32[128,8,128]{2,1,0:T(8,128)S(1)}, u32[]{:S(2)}, u32[]{:S(2)}) %all-to-all-start) | async-done | bytes 524320 | tf_op jit(solution)/shard_map/all_to_all | solution.py:366
  49.1 0.8 %copy-done = f32[128,8,128]{2,1,0:T(8,128)} copy-done((f32[128,8,128]{2,1,0:T(8,128)}, f32[128,8,128]{2,1,0:T(8,128)S(1)}, u32[]{:S(2)}) %copy-start) | copy-done | bytes 524312
  49.9 4.2 %filter.1 = f32[16,8,8,128]{3,2,1,0:T(8,128)} custom-call(f32[2]{0:T(128)} %pad_maximum_fusion.scalars, f32[16,8,8,128]{3,2,1,0:T(8,128)} %bitcast.15, bf16[2,512,512]{2,1,0:T(8,128)(2,1)} %constant.70.clone.matrix_y, bf16[2,256,256]{2,1,0:T(8,128)(2,1)} %constant.69.clone.matrix_x, f32[256,1]{1,0:T(8,128)} %constant.71.clone.terms_x, ...), custom_call_target="tpu_custom_call" | custom-call | tf_op jit(solution)/shard_map/filter/pallas_call | solution.py:379
  54.1 18.7 %all_to_all.10 = f32[128,8,128]{2,1,0:T(8,128)} all-to-all(f32[128,8,128]{2,1,0:T(8,128)} %bitcast.16), channel_id=1, replica_groups=mesh['gx'=16,'gy'=8] {'gx','gy'}, dimensions={0} | all-to-all | bytes 1048576 | tf_op jit(solution)/shard_map/all_to_all | solution.py:388
  72.9 2.4 %back.1 = f32[16,64,128]{2,1,0:T(8,128)} custom-call(f32[1024,128]{1,0:T(8,128)} %bitcast.14, bf16[2,128,128]{2,1,0:T(8,128)(2,1)} %constant.68.clone.forward_z.inverse_z, f32[16,64,128]{2,1,0:T(8,128)} %get-tuple-element.32.sample), custom_call_target="tpu_custom_call" | custom-call | tf_op jit(solution)/shard_map/back/pallas_call | solution.py:391
  (4 shorter events, 0.0 us)
Async XLA Ops:
  3.2 17.5 %collective-permute-start = (f32[2,4,64,128]{3,2,1,0:T(8,128)}, f32[2,4,64,128]{3,2,1,0:T(8,128)S(1)}, u32[]{:S(2)}, u32[]{:S(2)}) collective-permute-start(f32[2,4,64,128]{3,2,1,0:T(8,128)} %get-tuple-element.25), channel_id=1, source_target_pairs={{0,8},{8,16},{16,24},{24,32},{32,40},{40,48},{48,56},{56,64},{64,7... | collective-permute-start | bytes 786440 | tf_op jit(solution)/shard_map/ppermute | solution.py:315
  5.9 14.9 %collective-permute-start.1 = (f32[2,4,64,128]{3,2,1,0:T(8,128)}, f32[2,4,64,128]{3,2,1,0:T(8,128)S(1)}, u32[]{:S(2)}, u32[]{:S(2)}) collective-permute-start(f32[2,4,64,128]{3,2,1,0:T(8,128)} %get-tuple-element.26), channel_id=1, source_target_pairs={{8,0},{16,8},{24,16},{32,24},{40,32},{48,40},{56,48},{64,56},{72,6... | collective-permute-start | bytes 786440 | tf_op jit(solution)/shard_map/ppermute | solution.py:316
  5.9 14.8 %collective-permute-start.2 = (f32[2,8,8,128]{3,2,1,0:T(8,128)}, f32[2,8,8,128]{3,2,1,0:T(8,128)S(1)}, u32[]{:S(2)}, u32[]{:S(2)}) collective-permute-start(f32[2,8,8,128]{3,2,1,0:T(8,128)} %get-tuple-element.27), channel_id=1, source_target_pairs={{0,1},{1,2},{2,3},{3,4},{4,5},{5,6},{6,7},{7,0},{8,9},{9,10},{10,1... | collective-permute-start | bytes 196616 | tf_op jit(solution)/shard_map/ppermute | solution.py:317
  8.5 12.2 %collective-permute-start.3 = (f32[2,8,8,128]{3,2,1,0:T(8,128)}, f32[2,8,8,128]{3,2,1,0:T(8,128)S(1)}, u32[]{:S(2)}, u32[]{:S(2)}) collective-permute-start(f32[2,8,8,128]{3,2,1,0:T(8,128)} %get-tuple-element.28), channel_id=1, source_target_pairs={{1,0},{2,1},{3,2},{4,3},{5,4},{6,5},{7,6},{0,7},{9,8},{10,9},{11,1... | collective-permute-start | bytes 196616 | tf_op jit(solution)/shard_map/ppermute | solution.py:318
  11.6 0.7 copy-start.5
  11.6 0.7 copy-start.6
  20.7 0.6 copy-start.3
  20.7 0.6 copy-start.4
  20.7 0.7 copy-start.1
  20.7 0.8 %copy-start.2 = (f32[2,4,64,128]{3,2,1,0:T(8,128)}, f32[2,4,64,128]{3,2,1,0:T(8,128)S(1)}, u32[]{:S(2)}) copy-start(f32[2,4,64,128]{3,2,1,0:T(8,128)S(1)} %collective-permute-done.1.xhigh) | copy-start | bytes 786436
  25.2 23.9 %all-to-all-start = ((f32[128,8,128]{2,1,0:T(8,128)}), f32[128,8,128]{2,1,0:T(8,128)S(1)}, u32[]{:S(2)}, u32[]{:S(2)}) async-start(f32[128,8,128]{2,1,0:T(8,128)} %bitcast.17), calls=%async_computation | async-start | bytes 1048576 | tf_op jit(solution)/shard_map/all_to_all | solution.py:366
  35.7 0.7 copy-start.7
  49.1 0.8 %copy-start = (f32[128,8,128]{2,1,0:T(8,128)}, f32[128,8,128]{2,1,0:T(8,128)S(1)}, u32[]{:S(2)}) copy-start(f32[128,8,128]{2,1,0:T(8,128)S(1)} %all-to-all-done) | copy-start | bytes 1572868
where the time goes:
time: 75.7 us; the launch traced here: 75.3 us
  Pallas kernels  19.9 us (26%)
  blocking collectives  18.7 us (25%)
  starting transfers between devices  17.6 us (23%)
  waiting for transfers between devices  10.8 us (14%)
  local copies, waits for them, and re-layouts  4.14 us (5%)
  between operations  2.73 us (4%)
  other arithmetic  1.34 us (2%)
    all_to_all x1, blocking collectives, per_device(): lax.all_to_all(filtered.reshape(nz, 8, nz), ('gx', 'gy'), split_axis=0, c...  18.7 us
    all_to_all x1, waiting for transfers between devices, per_device(): lax.all_to_all(spectra.reshape(nz, 8, nz), ('gx', 'gy'), split_axis=0, co...  10.8 us
    all_to_all x1, starting transfers between devices, per_device(): lax.all_to_all(spectra.reshape(nz, 8, nz), ('gx', 'gy'), split_axis=0, co...  9.84 us
    pallas_call x1, Pallas kernels, per_device(): pl.pallas_call(local_kernel, out_shape=(block,) * 6 + (jax.ShapeDtypeStru...  7.04 us
    pallas_call x1, Pallas kernels, per_device(): pl.pallas_call(filter_kernel, out_shape=shape(parts_x, parts_y, 8, nz), i...  4.21 us
    pallas_call x1, Pallas kernels, per_device(): pl.pallas_call(finish_kernel, out_shape=(flat,) * 4, in_specs=[SMEM] * 4...  3.69 us
    unnamed x16, local copies, waits for them, and re-layouts  2.93 us
    ppermute x1, starting transfers between devices, per_device(): from_low_x = lax.ppermute(xhigh, 'gx', up_x)  2.67 us
  transfers between devices with their start and end apart: 5, of which 1 were waited for; matrix products, arithmetic and copies ran while one was open for 3% of the time, Pallas kernels for 9%

commit v1 on v0

v1 whole, which is shorter than its diff:
```python
import functools
import math

import jax
import jax.numpy as jnp
import numpy as np
from jax import lax
from jax.experimental import pallas as pl
from jax.experimental.pallas import tpu as pltpu
from jax.sharding import PartitionSpec as P

NSTEPS = 48
STENCIL_WEIGHTS = (-205.0 / 72.0, 8.0 / 5.0, -1.0 / 5.0, 8.0 / 315.0, -1.0 / 560.0)
COURANT_SQUARED = 0.08
VELOCITY_GAIN = 0.2
PULSE_FREQUENCY = 0.05
PULSE_AMPLITUDE = 20.0

F32 = jnp.float32
BF16 = jnp.bfloat16
ROW = (((1,), (0,)), ((), ()))
TRANSPOSED_RIGHT = (((1,), (1,)), ((), ()))
TRANSPOSED_LEFT = (((0,), (0,)), ((), ()))


def hartley(length):
    index = np.arange(length)
    angle = (index[:, None] * index[None, :] % length) * (2.0 * np.pi / length)
    return np.cos(angle) + np.sin(angle)


def halves(matrix):
    high = matrix.astype(np.float32).astype(jnp.bfloat16)
    low = (matrix - high.astype(np.float64)).astype(np.float32).astype(jnp.bfloat16)
    return np.stack([high, low])


def wave_terms(length):
    return (length / 8.0) ** 2 * 4.0 * np.sin(np.arange(length) * (np.pi / length)) ** 2


def band(length):
    matrix = np.zeros((length, length))
    for offset in range(5):
        weight = STENCIL_WEIGHTS[offset] * (3.0 if offset == 0 else 1.0)
        matrix += weight * np.eye(length, k=offset)
        if offset:
            matrix += weight * np.eye(length, k=-offset)
    return matrix


def split(value):
    high = value.astype(BF16)
    return high, (value - high.astype(F32)).astype(BF16)


def dot(left, right, dims=ROW):
    return lax.dot_general(left, right, dims, preferred_element_type=F32)


def dot_3(left, right, dims=ROW):
    total = dot(left[0], right[1], dims) + dot(left[1], right[0], dims)
    return total + dot(left[0], right[0], dims)


def edges_kernel(
    mean, logs, noise, adjoint, wave, xlow, xhigh, ylow, yhigh, ends, starts, stops, sems
):
    nx, ny, _ = wave.shape
    arrays = (mean, logs, noise, adjoint, wave)
    middle = slice(4, nx - 4)
    copies = []
    for i, array in enumerate(arrays):
        low, high = (xlow.at[0], xhigh.at[0]) if i == 4 else (ends.at[i, 0], ends.at[i, 1])
        copies.append(
            (
                pltpu.make_async_copy(array.at[0:4], low, sems.at[i, 0]),
                pltpu.make_async_copy(array.at[nx - 4 : nx], high, sems.at[i, 1]),
                pltpu.make_async_copy(array.at[middle, 0:8], starts.at[i], sems.at[i, 2]),
                pltpu.make_async_copy(array.at[middle, ny - 8 : ny], stops.at[i], sems.at[i, 3]),
            )
        )
    for part in range(4):
        for i in range(5):
            copies[i][part].start()

    def scaled(a, b, c, d):
        return COURANT_SQUARED * jnp.exp(2.0 * VELOCITY_GAIN * (a + jnp.exp(b) * c)) * d

    def pack(kind, base, first, last):
        for pair in range(first.shape[0] // 2):
            at = base // 2 + pair
            ylow[kind, at] = jnp.concatenate([first[2 * pair, 0:4], first[2 * pair + 1, 0:4]], 0)
            yhigh[kind, at] = jnp.concatenate([last[2 * pair, 4:8], last[2 * pair + 1, 4:8]], 0)

    for part, (side, base) in enumerate(((xlow, 0), (xhigh, nx - 4))):
        for i in range(5):
            copies[i][part].wait()
        side[1] = scaled(*(ends[i, part] for i in range(4)))
        for kind in range(2):
            pack(kind, base, side[kind, :, 0:8], side[kind, :, ny - 8 : ny])
    for part in range(2, 4):
        for i in range(5):
            copies[i][part].wait()
    pack(0, 4, starts[4], stops[4])
    pack(1, 4, scaled(*(starts[i] for i in range(4))), scaled(*(stops[i] for i in range(4))))


def local_kernel(
    sources_from, receivers_from, observed_from, wave_prev_from, adjoint_next_from, bands_from,
    mean, logs, noise, wave, adjoint,
    curved, base_wave, base_adjoint, speed, tilt, codes, records, counts,
    field, plane, sources, receivers, observed, wave_prev, adjoint_next, bands, sems,
):
    nx, ny, nz = wave.shape
    index_x, index_y = lax.axis_index("gx"), lax.axis_index("gy")
    n_sources, n_receivers = sources.shape[1], receivers.shape[1]
    copies = [
        pltpu.make_async_copy(sources_from, sources, sems.at[0]),
        pltpu.make_async_copy(receivers_from, receivers, sems.at[1]),
        pltpu.make_async_copy(observed_from, observed, sems.at[2]),
        pltpu.make_async_copy(wave_prev_from, wave_prev, sems.at[3]),
        pltpu.make_async_copy(adjoint_next_from, adjoint_next, sems.at[4]),
        pltpu.make_async_copy(bands_from, bands, sems.at[5]),
    ]
    for copy in copies:
        copy.start()

    def scan(points, start, number, at, count, recorded):
        for i in range(number):
            mine_x = points[0, start + i] - index_x * nx
            mine_y = points[1, start + i] - index_y * ny
            inside = (mine_x >= 0) & (mine_x < nx) & (mine_y >= 0) & (mine_y < ny)
            codes[at + count] = (mine_x * ny + mine_y) * nz + points[2, start + i]
            if recorded:
                records[count] = observed[start + i]
            count = count + inside.astype(jnp.int32)
        return count

    for kind in range(2):
        field[kind, 0:4] = jnp.zeros((4, ny + 16, nz), F32)
        field[kind, nx + 4 : nx + 8] = jnp.zeros((4, ny + 16, nz), F32)
        field[kind, :, 0:8] = jnp.zeros((nx + 8, 8, nz), F32)
        field[kind, :, ny + 8 : ny + 16] = jnp.zeros((nx + 8, 8, nz), F32)

    def prepare(x, _):
        spread_noise = jnp.exp(logs[x]) * noise[x]
        value = mean[x] + spread_noise
        rate = COURANT_SQUARED * jnp.exp(2.0 * VELOCITY_GAIN * value)
        tilt[x] = spread_noise
        speed[x] = rate
        field[0, x + 4, 8 : ny + 8] = wave[x]
        field[1, x + 4, 8 : ny + 8] = rate * adjoint[x]
        return 0

    lax.fori_loop(0, nx, prepare, 0)

    copies[5].wait()
    for kind in range(2):
        value = field[kind, 4 : nx + 4, 8 : ny + 8].reshape(nx * ny, nz)
        plane[kind] = lax.dot_general(
            value, bands[...], ROW, precision=lax.Precision.HIGHEST, preferred_element_type=F32
        )

    def lateral(kind, x):
        total = plane[kind, pl.ds(pl.multiple_of(x * ny, ny), ny)]
        for offset in range(1, 5):
            near = field[kind, x + 4 + offset, 8 : ny + 8] + field[kind, x + 4 - offset, 8 : ny + 8]
            near = near + field[kind, x + 4, 8 + offset : ny + 8 + offset]
            near = near + field[kind, x + 4, 8 - offset : ny + 8 - offset]
            total = total + STENCIL_WEIGHTS[offset] * near
        return total

    for copy in copies[:5]:
        copy.wait()

    def finish(x, count):
        bend = lateral(0, x)
        curved[x] = bend
        base_wave[x] = 2.0 * wave[x] - wave_prev[x] + speed[x] * bend
        base_adjoint[x] = 2.0 * adjoint[x] - adjoint_next[x] + lateral(1, x)
        step = n_sources // nx
        some = scan(sources, x * step, step, 0, count[0], False)
        step = n_receivers // nx
        return some, scan(receivers, x * step, step, n_sources + 1, count[1], True)

    found = lax.fori_loop(0, nx, finish, (jnp.int32(0), jnp.int32(0)))
    counts[0], counts[1] = found


def finish_kernel(
    codes, records, counts, step_index,
    curved, base_wave, base_adjoint, speed, tilt,
    xlow, xhigh, ylow, yhigh, forward_z,
    wave_to, adjoint_to, logscale_to, spectra_to,
    wave_next, adjoint_prev, logscale_grad, slope, spectra, sems,
):
    nx, ny, nz = curved.shape
    index_x, index_y = lax.axis_index("gx"), lax.axis_index("gy")
    n_sources = codes.shape[0] - records.shape[0] - 1
    row_at = lax.broadcasted_iota(jnp.int32, (8, nz), 0)
    lane_at = lax.broadcasted_iota(jnp.int32, (1, nz), 1)
    keep = [
        index_x > 0,
        index_x < lax.axis_size("gx") - 1,
        index_y > 0,
        index_y < lax.axis_size("gy") - 1,
    ]
    keep = [value.astype(F32) for value in keep]
    moment = jnp.full((1, nz), step_index[0] - NSTEPS // 2).astype(F32)
    moment = moment * (math.pi * PULSE_FREQUENCY)
    pulse = PULSE_AMPLITUDE * (1.0 - 2.0 * moment * moment) * jnp.exp(-moment * moment)

    def lateral_y(kind, x):
        start = jnp.zeros((8, nz), F32)
        end = jnp.zeros((8, nz), F32)
        low, high = ylow[kind, x // 2], yhigh[kind, x // 2]
        mine = row_at < 4 if x % 2 == 0 else row_at >= 4
        low, high = jnp.where(mine, low, 0.0), jnp.where(mine, high, 0.0)
        base = 0 if x % 2 == 0 else 4
        for offset in range(1, 5):
            start = start + STENCIL_WEIGHTS[offset] * pltpu.roll(low, (offset - 4 - base) % 8, 0)
            end = end + STENCIL_WEIGHTS[offset] * pltpu.roll(high, (8 - offset - base) % 8, 0)
        return jnp.where(row_at < 4, start, 0.0) * keep[2], jnp.where(row_at >= 4, end, 0.0) * keep[3]

    def change(kind, x):
        start, end = lateral_y(kind, x)
        total = jnp.concatenate([start, jnp.zeros((ny - 16, nz), F32), end], 0)
        side = None
        for offset in range(1, 5):
            if x - offset < 0:
                term = STENCIL_WEIGHTS[offset] * keep[0] * xlow[kind, x - offset + 4]
            elif x + offset >= nx:
                term = STENCIL_WEIGHTS[offset] * keep[1] * xhigh[kind, x + offset - nx]
            else:
                continue
            total = total + term
        return total

    for x in range(nx):
        more = change(0, x)
        bend = curved[x] + more
        rows = slice(x * ny, (x + 1) * ny)
        wave_next[rows] = base_wave[x] + speed[x] * more
        adjoint_prev[rows] = base_adjoint[x] + change(1, x)
        slope[rows] = (2.0 * VELOCITY_GAIN) * speed[x] * bend

    def place(at):
        return pl.ds(codes[at] // nz, 1), lane_at == codes[at] % nz

    def shoot(i, _):
        row, hit = place(i)
        wave_next[row] = wave_next[row] + jnp.where(hit, pulse, 0.0)
        return 0

    lax.fori_loop(0, counts[0], shoot, 0)

    def record(i, _):
        row, hit = place(n_sources + 1 + i)
        misfit = wave_next[row] - records[i]
        adjoint_prev[row] = adjoint_prev[row] + jnp.where(hit, misfit, 0.0)
        return 0

    lax.fori_loop(0, counts[1], record, 0)

    copies = [
        pltpu.make_async_copy(wave_next, wave_to, sems.at[0]),
        pltpu.make_async_copy(adjoint_prev, adjoint_to, sems.at[1]),
    ]
    for copy in copies:
        copy.start()
    matrix = (forward_z[0], forward_z[1])
    for j in range(nx // 2):
        rows = slice(2 * j * ny, 2 * (j + 1) * ny)
        grad = slope[rows] * adjoint_prev[rows]
        logscale_grad[rows] = grad * tilt[2 * j : 2 * j + 2].reshape(2 * ny, nz) - 1.0
        spectra[pl.ds(j, nz, stride=8)] = dot_3(matrix, split(grad), TRANSPOSED_RIGHT)
        copy = pltpu.make_async_copy(logscale_grad.at[rows], logscale_to.at[rows], sems.at[3 + j])
        copy.start()
        copies.append(copy)
    copies.append(pltpu.make_async_copy(spectra, spectra_to, sems.at[2]))
    copies[-1].start()
    for copy in copies:
        copy.wait()


def gain_kernel(
    prior_scale, terms_z, after, matrix_y_from, matrix_x_from, mean_from, terms_x, terms_y, tilt,
    gain, matrix_y, matrix_x, sample, sems,
):
    copies = [
        pltpu.make_async_copy(matrix_y_from, matrix_y, sems.at[0]),
        pltpu.make_async_copy(matrix_x_from, matrix_x, sems.at[1]),
        pltpu.make_async_copy(mean_from, sample, sems.at[2]),
    ]
    for copy in copies:
        copy.start()
    depth = lax.axis_index("gx") * lax.axis_size("gy") + lax.axis_index("gy")
    cells = gain.shape[0] * gain.shape[1] * terms_z.shape[0]
    scale = prior_scale[0] * (math.sqrt(cells) / 8.0 / cells)
    gain[...] = scale / (((1.0 + terms_z[depth]) + terms_x[...]) + terms_y[...])
    for copy in copies:
        copy.wait()
    sample[...] = sample[...] + tilt[...]


def filter_kernel(spectra, matrix_y, matrix_x, gain, result, plane):
    half = plane.shape[0] // 2
    tiles_x, tiles_y = spectra.shape[0], spectra.shape[1]
    lane = lax.broadcasted_iota(jnp.int32, (half, 128), 1)
    for m in range(tiles_y // 2):
        even = spectra[:, 2 * m].reshape(half, 128)
        odd = spectra[:, 2 * m + 1].reshape(half, 128)
        columns = slice(128 * m, 128 * (m + 1))
        plane[0:half, columns] = jnp.where(lane < 64, even, pltpu.roll(odd, 64, 1))
        plane[half:, columns] = jnp.where(lane < 64, pltpu.roll(even, 64, 1), odd)
    pair_y = (matrix_y[0], matrix_y[1])
    pair_x = (matrix_x[0], matrix_x[1])
    value = dot_3(split(plane[...]), pair_y)
    value = dot_3(pair_x, split(value))
    value = value * gain[...]
    value = dot_3(pair_x, split(value), TRANSPOSED_LEFT)
    plane[...] = dot_3(split(value), pair_y)
    for m in range(tiles_y // 2):
        columns = slice(128 * m, 128 * (m + 1))
        even, odd = plane[0:half, columns], plane[half:, columns]
        first = jnp.where(lane < 64, even, pltpu.roll(odd, 64, 1))
        second = jnp.where(lane < 64, pltpu.roll(even, 64, 1), odd)
        result[:, 2 * m] = first.reshape(tiles_x, 8, 128)
        result[:, 2 * m + 1] = second.reshape(tiles_x, 8, 128)


def back_kernel(spectra, inverse_z, sample, search_to, search, sems):
    nx, ny, nz = sample.shape
    matrix = (inverse_z[0], inverse_z[1])
    copies = []
    for j in range(nx // 2):
        value = split(spectra[pl.ds(j, nz, stride=8)])
        smooth = dot_3(value, matrix, TRANSPOSED_LEFT)
        pair = slice(2 * j, 2 * j + 2)
        search[pair] = smooth.reshape(2, ny, nz) + sample[pair]
        copies.append(pltpu.make_async_copy(search.at[pair], search_to.at[pair], sems.at[j]))
        copies[-1].start()
    for copy in copies:
        copy.wait()


SMEM = pl.BlockSpec(memory_space=pltpu.SMEM)
VMEM = pl.BlockSpec(memory_space=pltpu.VMEM)
HBM = pl.BlockSpec(memory_space=pltpu.HBM)


def far(*sizes):
    return jax.ShapeDtypeStruct(sizes, F32)


def near(*sizes):
    return pltpu.VMEM(sizes, F32)


def call(kernel, scalars, stay, arrays, out_shape, out_specs, scratch, name):
    stay = [pltpu.with_memory_space_constraint(value, pltpu.HBM) for value in stay]
    arrays = [pltpu.with_memory_space_constraint(value, pltpu.VMEM) for value in arrays]
    return pl.pallas_call(
        kernel,
        out_shape=out_shape,
        in_specs=[SMEM] * len(scalars) + [HBM] * len(stay) + [VMEM] * len(arrays),
        out_specs=out_specs,
        scratch_shapes=scratch,
        compiler_params=pltpu.CompilerParams(vmem_limit_bytes=16 << 20),
        name=name,
    )(*scalars, *stay, *arrays)


def per_device(
    mean_field,
    log_scale,
    noise,
    wave_prev,
    wave_now,
    adjoint_next,
    adjoint_now,
    sources,
    receivers,
    observed,
    step_index,
    prior_scale,
):
    nx, ny, nz = wave_now.shape
    parts_x, parts_y = lax.axis_size("gx"), lax.axis_size("gy")
    total_x, total_y = nx * parts_x, ny * parts_y
    block = near(nx, ny, nz)
    flat = near(nx * ny, nz)

    edge = near(2, 4, ny, nz), near(2, nx // 2, 8, nz)
    xlow, xhigh, ylow, yhigh = call(
        edges_kernel,
        (),
        (mean_field, log_scale, noise, adjoint_now, wave_now),
        (),
        (edge[0], edge[0], edge[1], edge[1]),
        (VMEM,) * 4,
        [
            near(4, 2, 4, ny, nz),
            near(5, nx - 8, 8, nz),
            near(5, nx - 8, 8, nz),
            pltpu.SemaphoreType.DMA((5, 4)),
        ],
        "edges",
    )

    up_x = [(i, (i + 1) % parts_x) for i in range(parts_x)]
    down_x = [(j, i) for i, j in up_x]
    up_y = [(i, (i + 1) % parts_y) for i in range(parts_y)]
    down_y = [(j, i) for i, j in up_y]
    from_low_x = lax.ppermute(xhigh, "gx", up_x)
    from_high_x = lax.ppermute(xlow, "gx", down_x)
    from_low_y = lax.ppermute(yhigh, "gy", up_y)
    from_high_y = lax.ppermute(ylow, "gy", down_y)

    sources, receivers = sources.T, receivers.T
    n_sources, n_receivers = sources.shape[1], receivers.shape[1]
    bands = jnp.asarray(band(nz).astype(np.float32))
    curved, base_wave, base_adjoint, speed, tilt, codes, records, counts = call(
        local_kernel,
        (),
        (sources, receivers, observed, wave_prev, adjoint_next, bands),
        (mean_field, log_scale, noise, wave_now, adjoint_now),
        (block,) * 5
        + (
            jax.ShapeDtypeStruct((n_sources + n_receivers + 2,), jnp.int32),
            jax.ShapeDtypeStruct((n_receivers + 1,), F32),
            jax.ShapeDtypeStruct((2,), jnp.int32),
        ),
        (VMEM,) * 5 + (SMEM,) * 3,
        [
            near(2, nx + 8, ny + 16, nz),
            near(2, nx * ny, nz),
            pltpu.SMEM(sources.shape, jnp.int32),
            pltpu.SMEM(receivers.shape, jnp.int32),
            pltpu.SMEM(observed.shape, F32),
            near(nx, ny, nz),
            near(nx, ny, nz),
            near(nz, nz),
            pltpu.SemaphoreType.DMA((6,)),
        ],
        "local",
    )

    matrix_z = jnp.asarray(halves(hartley(nz)))
    wave_next, adjoint_prev, logscale_grad, spectra = call(
        finish_kernel,
        (codes, records, counts, step_index),
        (),
        (
            curved, base_wave, base_adjoint, speed, tilt,
            from_low_x, from_high_x, from_low_y, from_high_y, matrix_z,
        ),
        (pltpu.HBM((nx * ny, nz), F32),) * 4,
        (HBM,) * 4,
        [flat] * 5 + [pltpu.SemaphoreType.DMA((3 + nx // 2,))],
        "finish",
    )

    spectra = lax.all_to_all(
        spectra.reshape(nz, 8, nz), ("gx", "gy"), split_axis=0, concat_axis=0, tiled=True
    )

    order = np.arange(total_x).reshape(parts_x, nx // 2, 2).transpose(2, 0, 1).reshape(-1)
    matrix_x = jnp.asarray(halves(hartley(total_x)[:, order]))
    matrix_y = jnp.asarray(halves(hartley(total_y)))
    terms_x = jnp.asarray(wave_terms(total_x).astype(np.float32)[:, None])
    terms_y = jnp.asarray(wave_terms(total_y).astype(np.float32)[None, :])
    terms_z = jnp.asarray(wave_terms(nz).astype(np.float32))
    gain, matrix_y, matrix_x, sample = call(
        gain_kernel,
        (prior_scale, terms_z),
        (logscale_grad, matrix_y, matrix_x, mean_field),
        (terms_x, terms_y, tilt),
        (
            near(total_x, total_y),
            pltpu.VMEM(matrix_y.shape, BF16),
            pltpu.VMEM(matrix_x.shape, BF16),
            block,
        ),
        (VMEM,) * 4,
        [pltpu.SemaphoreType.DMA((3,))],
        "gain",
    )
    filtered = call(
        filter_kernel,
        (),
        (),
        (spectra.reshape(parts_x, parts_y, 8, nz), matrix_y, matrix_x, gain),
        far(parts_x, parts_y, 8, nz),
        VMEM,
        [near(total_x, total_y)],
        "filter",
    )

    filtered = lax.all_to_all(
        filtered.reshape(nz, 8, nz), ("gx", "gy"), split_axis=0, concat_axis=0, tiled=True
    )
    search = call(
        back_kernel,
        (),
        (),
        (filtered.reshape(nx * ny, nz), matrix_z, sample),
        pltpu.HBM((nx, ny, nz), F32),
        HBM,
        [block, pltpu.SemaphoreType.DMA((nx // 2,))],
        "back",
    )
    return (
        wave_next.reshape(nx, ny, nz),
        adjoint_prev.reshape(nx, ny, nz),
        search,
        logscale_grad.reshape(nx, ny, nz),
    )


def solution(mesh):
    grid = P("gx", "gy", None)
    return jax.shard_map(
        per_device,
        mesh=mesh,
        in_specs=(grid,) * 7 + (P(),) * 5,
        out_specs=(grid,) * 4,
        check_vma=False,
    )
```

time: 75.7 us -> 64.4 us (0.85)
  Pallas kernels: 19.9 us -> 15.2 us
  local copies, waits for them, and re-layouts: 4.14 us -> 1.58 us
  other arithmetic: 1.34 us -> 0 us
  waiting for transfers between devices: 10.8 us -> 9.75 us
  blocking collectives: 18.7 us -> 17.7 us
    pallas_call x5 -> x6, Pallas kernels: 19.9 us -> 15.2 us  [call(): pl.pallas_call(kernel, out_shape=out_shape, in_specs=[SMEM] * len(scalars...]
    unnamed x16 -> x18, local copies, waits for them, and re-layouts: 2.93 us -> 1.58 us
    all_to_all x1, waiting for transfers between devices: 10.8 us -> 9.74 us  [per_device(): lax.all_to_all(spectra.reshape(nz, 8, nz), ('gx', 'gy'), split_axis=0, co...]
    all_to_all x1, blocking collectives: 18.7 us -> 17.7 us  [per_device(): lax.all_to_all(filtered.reshape(nz, 8, nz), ('gx', 'gy'), split_axis=0, c...]
  transfers between devices with their start and end apart: 5 -> 5, of which waited for: 1 -> 1; matrix products, arithmetic and copies ran while one was open for 3% -> 0% of each run, Pallas kernels for 9% -> 12%
where the time goes in v1:
time: 64.4 us; the launch traced here: 64.1 us
  starting transfers between devices  17.7 us (27%)
  blocking collectives  17.7 us (27%)
  Pallas kernels  15.2 us (24%)
  waiting for transfers between devices  9.75 us (15%)
  between operations  2.14 us (3%)
  local copies, waits for them, and re-layouts  1.58 us (2%)
    all_to_all x1, blocking collectives, per_device(): lax.all_to_all(filtered.reshape(nz, 8, nz), ('gx', 'gy'), split_axis=0, c...  17.7 us
    pallas_call x6, Pallas kernels, call(): pl.pallas_call(kernel, out_shape=out_shape, in_specs=[SMEM] * len(scalars...  15.2 us
    all_to_all x1, starting transfers between devices, per_device(): lax.all_to_all(spectra.reshape(nz, 8, nz), ('gx', 'gy'), split_axis=0, co...  9.89 us
    all_to_all x1, waiting for transfers between devices, per_device(): lax.all_to_all(spectra.reshape(nz, 8, nz), ('gx', 'gy'), split_axis=0, co...  9.74 us
    ppermute x1, starting transfers between devices, per_device(): from_low_x = lax.ppermute(xhigh, 'gx', up_x)  2.74 us
    ppermute x1, starting transfers between devices, per_device(): from_low_y = lax.ppermute(yhigh, 'gy', up_y)  2.62 us
    ppermute x1, starting transfers between devices, per_device(): from_high_y = lax.ppermute(ylow, 'gy', down_y)  2.46 us
    unnamed x18, local copies, waits for them, and re-layouts  1.58 us
  transfers between devices with their start and end apart: 5, of which 1 were waited for; matrix products, arithmetic and copies ran while one was open for 0% of the time, Pallas kernels for 12%

profile of v1, /device:TPU:1, one launch (start us, length us, event | category | flops | bytes accessed | tf_op | source)
XLA Modules:
  0.0 64.1 jit_solution(886139332006910166)
XLA Ops:
  0.6 0.0 copy-start
  0.6 0.0 copy-start.1
  0.7 0.0 copy-start.2
  0.7 0.0 copy-start.3
  0.7 0.0 copy-start.4
  0.7 1.8 %edges.1 = (f32[2,4,64,128]{3,2,1,0:T(8,128)S(1)}, f32[2,4,64,128]{3,2,1,0:T(8,128)S(1)}, f32[2,8,8,128]{3,2,1,0:T(8,128)S(1)}, f32[2,8,8,128]{3,2,1,0:T(8,128)S(1)}) custom-call(f32[16,64,128]{2,1,0:T(8,128)} %mean_from.1, f32[16,64,128]{2,1,0:T(8,128)} %logs.3, f32[16,64,128]{2,1,0:T(8,128)} %noise.3, f32[16,64,128]{2,1,0:T(8,128)} %adjoint.3, ...), custom_call_target="tpu_custom_call" | custom-call | tf_op jit(solution)/shard_map/edges/pallas_call | solution.py:364
  2.5 2.7 %collective-permute-start = (f32[2,4,64,128]{3,2,1,0:T(8,128)S(1)}, f32[2,4,64,128]{3,2,1,0:T(8,128)S(1)}, u32[]{:S(2)}, u32[]{:S(2)}) collective-permute-start(f32[2,4,64,128]{3,2,1,0:T(8,128)S(1)} %get-tuple-element.32), channel_id=1, source_target_pairs={{0,8},{8,16},{16,24},{24,32},{32,40},{40,48},{48,56},{56,64},{64,7... | collective-permute-start | bytes 786440 | tf_op jit(solution)/shard_map/ppermute | solution.py:416
  5.2 0.0 collective-permute-start.1
  5.2 2.6 %collective-permute-start.2 = (f32[2,8,8,128]{3,2,1,0:T(8,128)S(1)}, f32[2,8,8,128]{3,2,1,0:T(8,128)S(1)}, u32[]{:S(2)}, u32[]{:S(2)}) collective-permute-start(f32[2,8,8,128]{3,2,1,0:T(8,128)S(1)} %get-tuple-element.34), channel_id=1, source_target_pairs={{0,1},{1,2},{2,3},{3,4},{4,5},{5,6},{6,7},{7,0},{8,9},{9,10},{10,1... | collective-permute-start | bytes 196616 | tf_op jit(solution)/shard_map/ppermute | solution.py:418
  7.8 2.5 %collective-permute-start.3 = (f32[2,8,8,128]{3,2,1,0:T(8,128)S(1)}, f32[2,8,8,128]{3,2,1,0:T(8,128)S(1)}, u32[]{:S(2)}, u32[]{:S(2)}) collective-permute-start(f32[2,8,8,128]{3,2,1,0:T(8,128)S(1)} %get-tuple-element.35), channel_id=1, source_target_pairs={{1,0},{2,1},{3,2},{4,3},{5,4},{6,5},{7,6},{0,7},{9,8},{10,9},{11,1... | collective-permute-start | bytes 196616 | tf_op jit(solution)/shard_map/ppermute | solution.py:419
  11.0 0.0 copy-done
  11.0 0.0 copy-done.1
  11.0 0.0 copy-done.2
  11.0 0.0 copy-done.3
  11.0 0.0 copy-done.4
  11.0 0.0 copy-start.5
  11.0 5.7 %local.1 = (f32[16,64,128]{2,1,0:T(8,128)S(1)}, f32[16,64,128]{2,1,0:T(8,128)S(1)}, f32[16,64,128]{2,1,0:T(8,128)S(1)}, f32[16,64,128]{2,1,0:T(8,128)S(1)}, f32[...) custom-call(s32[3,16]{1,0:T(4,128)} %bitcast.15, s32[3,256]{1,0:T(4,128)} %bitcast.14, ...), custom_call_target="tpu_custom_call" | custom-call | tf_op jit(solution)/shard_map/local/pallas_call | solution.py:364
  16.7 0.0 collective-permute-done.2.ylow
  16.8 0.0 collective-permute-done.3.yhigh
  16.8 0.0 collective-permute-done.xlow
  16.8 0.0 collective-permute-done.1.xhigh
  16.8 2.6 %finish.1 = (f32[1024,128]{1,0:T(8,128)}, f32[1024,128]{1,0:T(8,128)}, f32[1024,128]{1,0:T(8,128)}, f32[1024,128]{1,0:T(8,128)}) custom-call(s32[274]{0:T(512)S(1)} %get-tuple-element.24.codes, f32[257]{0:T(512)S(1)} %get-tuple-element.25.records, s32[2]{0:T(128)S(1)} %get-tuple-element.26.counts, s32[1]{0:T(128)S(6)} %copy.23.step_index, ...), custom_call_target="tpu_custom_call" | custom-call | tf_op jit(solution)/shard_map/finish/pallas_call | solution.py:364
  19.4 9.9 %all-to-all-start = ((f32[128,8,128]{2,1,0:T(8,128)}), f32[128,8,128]{2,1,0:T(8,128)S(1)}, u32[]{:S(2)}, u32[]{:S(2)}) async-start(f32[128,8,128]{2,1,0:T(8,128)} %bitcast.13), calls=%async_computation | async-start | bytes 1048576 | tf_op jit(solution)/shard_map/all_to_all | solution.py:465
  29.3 0.0 copy-start.7
  30.0 0.0 copy-start.8
  30.0 0.6 copy-done.8
  30.6 0.9 %copy-done.6 = f32[256,1]{1,0:T(8,128)S(1)} copy-done((f32[256,1]{1,0:T(8,128)S(1)}, f32[256,1]{1,0:T(8,128)}, u32[]{:S(2)}) %copy-start.6) | copy-done | bytes 1048
  31.5 2.1 %gain.1 = (f32[256,512]{1,0:T(8,128)S(1)}, bf16[2,512,512]{2,1,0:T(8,128)(2,1)S(1)}, bf16[2,256,256]{2,1,0:T(8,128)(2,1)S(1)}, f32[16,64,128]{2,1,0:T(8,128)S(1)}) custom-call(f32[1]{0:T(128)S(6)} %copy.24.prior_scale, f32[128]{0:T(128)S(1)} %copy-done.8, f32[1024,128]{1,0:T(8,128)} %get-tuple-element.39.after, ...), custom_call_target="tpu_custom_call" | custom-call | tf_op jit(solution)/shard_map/gain/pallas_call | solution.py:364
  33.6 9.7 %all-to-all-done = f32[128,8,128]{2,1,0:T(8,128)S(1)} async-done(((f32[128,8,128]{2,1,0:T(8,128)}), f32[128,8,128]{2,1,0:T(8,128)S(1)}, u32[]{:S(2)}, u32[]{:S(2)}) %all-to-all-start) | async-done | bytes 524320 | tf_op jit(solution)/shard_map/all_to_all | solution.py:465
  43.3 1.9 %filter.1 = f32[16,8,8,128]{3,2,1,0:T(8,128)S(1)} custom-call(f32[16,8,8,128]{3,2,1,0:T(8,128)S(1)} %bitcast.10, bf16[2,512,512]{2,1,0:T(8,128)(2,1)S(1)} %get-tuple-element.40.matrix_y, bf16[2,256,256]{2,1,0:T(8,128)(2,1)S(1)} %get-tuple-element.41.matrix_x, f32[256,512]{1,0:T(8,128)S(1)} %get-tuple-element.42.gain), custom_call_target="tpu_custom_call" | custom-call | tf_op jit(solution)/shard_map/filter/pallas_call | solution.py:364
  45.3 17.7 %all_to_all.10 = f32[128,8,128]{2,1,0:T(8,128)S(1)} all-to-all(f32[128,8,128]{2,1,0:T(8,128)S(1)} %bitcast.11), channel_id=1, replica_groups=mesh['gx'=16,'gy'=8] {'gx','gy'}, dimensions={0} | all-to-all | bytes 1048576 | tf_op jit(solution)/shard_map/all_to_all | solution.py:501
  63.0 1.1 %back.1 = f32[16,64,128]{2,1,0:T(8,128)} custom-call(f32[1024,128]{1,0:T(8,128)S(1)} %bitcast.9, bf16[2,128,128]{2,1,0:T(8,128)(2,1)S(1)} %copy-done.5, f32[16,64,128]{2,1,0:T(8,128)S(1)} %get-tuple-element.43.sample), custom_call_target="tpu_custom_call" | custom-call | tf_op jit(solution)/shard_map/back/pallas_call | solution.py:364
  (3 shorter events, 0.0 us)
Async XLA Ops:
  0.6 10.3 %copy-start = (f32[16,64,128]{2,1,0:T(8,128)S(1)}, f32[16,64,128]{2,1,0:T(8,128)}, u32[]{:S(2)}) copy-start(f32[16,64,128]{2,1,0:T(8,128)} %mean_from.1) | copy-start | bytes 1572868
  0.6 10.3 %copy-start.1 = (f32[16,64,128]{2,1,0:T(8,128)S(1)}, f32[16,64,128]{2,1,0:T(8,128)}, u32[]{:S(2)}) copy-start(f32[16,64,128]{2,1,0:T(8,128)} %logs.3) | copy-start | bytes 1572868
  0.7 10.3 %copy-start.2 = (f32[16,64,128]{2,1,0:T(8,128)S(1)}, f32[16,64,128]{2,1,0:T(8,128)}, u32[]{:S(2)}) copy-start(f32[16,64,128]{2,1,0:T(8,128)} %noise.3) | copy-start | bytes 1572868
  0.7 10.3 %copy-start.3 = (f32[16,64,128]{2,1,0:T(8,128)S(1)}, f32[16,64,128]{2,1,0:T(8,128)}, u32[]{:S(2)}) copy-start(f32[16,64,128]{2,1,0:T(8,128)} %wave.3) | copy-start | bytes 1572868
  0.7 10.3 %copy-start.4 = (f32[16,64,128]{2,1,0:T(8,128)S(1)}, f32[16,64,128]{2,1,0:T(8,128)}, u32[]{:S(2)}) copy-start(f32[16,64,128]{2,1,0:T(8,128)} %adjoint.3) | copy-start | bytes 1572868
  2.5 14.3 %collective-permute-start = (f32[2,4,64,128]{3,2,1,0:T(8,128)S(1)}, f32[2,4,64,128]{3,2,1,0:T(8,128)S(1)}, u32[]{:S(2)}, u32[]{:S(2)}) collective-permute-start(f32[2,4,64,128]{3,2,1,0:T(8,128)S(1)} %get-tuple-element.32), channel_id=1, source_target_pairs={{0,8},{8,16},{16,24},{24,32},{32,40},{40,48},{48,56},{56,64},{64,7... | collective-permute-start | bytes 786440 | tf_op jit(solution)/shard_map/ppermute | solution.py:416
  5.2 11.6 %collective-permute-start.1 = (f32[2,4,64,128]{3,2,1,0:T(8,128)S(1)}, f32[2,4,64,128]{3,2,1,0:T(8,128)S(1)}, u32[]{:S(2)}, u32[]{:S(2)}) collective-permute-start(f32[2,4,64,128]{3,2,1,0:T(8,128)S(1)} %get-tuple-element.33), channel_id=1, source_target_pairs={{8,0},{16,8},{24,16},{32,24},{40,32},{48,40},{56,48},{64,56},{72,6... | collective-permute-start | bytes 786440 | tf_op jit(solution)/shard_map/ppermute | solution.py:417
  5.2 11.5 %collective-permute-start.2 = (f32[2,8,8,128]{3,2,1,0:T(8,128)S(1)}, f32[2,8,8,128]{3,2,1,0:T(8,128)S(1)}, u32[]{:S(2)}, u32[]{:S(2)}) collective-permute-start(f32[2,8,8,128]{3,2,1,0:T(8,128)S(1)} %get-tuple-element.34), channel_id=1, source_target_pairs={{0,1},{1,2},{2,3},{3,4},{4,5},{5,6},{6,7},{7,0},{8,9},{9,10},{10,1... | collective-permute-start | bytes 196616 | tf_op jit(solution)/shard_map/ppermute | solution.py:418
  7.8 8.9 %collective-permute-start.3 = (f32[2,8,8,128]{3,2,1,0:T(8,128)S(1)}, f32[2,8,8,128]{3,2,1,0:T(8,128)S(1)}, u32[]{:S(2)}, u32[]{:S(2)}) collective-permute-start(f32[2,8,8,128]{3,2,1,0:T(8,128)S(1)} %get-tuple-element.35), channel_id=1, source_target_pairs={{1,0},{2,1},{3,2},{4,3},{5,4},{6,5},{7,6},{0,7},{9,8},{10,9},{11,1... | collective-permute-start | bytes 196616 | tf_op jit(solution)/shard_map/ppermute | solution.py:419
  11.0 5.8 %copy-start.5 = (bf16[2,128,128]{2,1,0:T(8,128)(2,1)S(1)}, bf16[2,128,128]{2,1,0:T(8,128)(2,1)}, u32[]{:S(2)}) copy-start(bf16[2,128,128]{2,1,0:T(8,128)(2,1)} %constant.15.clone.forward_z.inverse_z) | copy-start | bytes 196612
  19.4 23.9 %all-to-all-start = ((f32[128,8,128]{2,1,0:T(8,128)}), f32[128,8,128]{2,1,0:T(8,128)S(1)}, u32[]{:S(2)}, u32[]{:S(2)}) async-start(f32[128,8,128]{2,1,0:T(8,128)} %bitcast.13), calls=%async_computation | async-start | bytes 1048576 | tf_op jit(solution)/shard_map/all_to_all | solution.py:465
  29.3 0.7 %copy-start.7 = (f32[1,512]{1,0:T(1,128)S(1)}, f32[1,512]{1,0:T(1,128)}, u32[]{:S(2)}) copy-start(f32[1,512]{1,0:T(1,128)} %constant.19.clone.terms_y) | copy-start | bytes 6148
  30.0 0.7 %copy-start.8 = (f32[128]{0:T(128)S(1)}, f32[128]{0:T(128)}, u32[]{:S(2)}) copy-start(f32[128]{0:T(128)} %constant.20.clone.terms_z) | copy-start | bytes 1540
  30.6 0.9 %copy-start.6 = (f32[256,1]{1,0:T(8,128)S(1)}, f32[256,1]{1,0:T(8,128)}, u32[]{:S(2)}) copy-start(f32[256,1]{1,0:T(8,128)} %constant.18.clone.terms_x) | copy-start | bytes 3076

commit v2 on v1

v2 whole, which is shorter than its diff:
```python
import functools
import math

import jax
import jax.numpy as jnp
import numpy as np
from jax import lax
from jax.experimental import pallas as pl
from jax.experimental.pallas import tpu as pltpu
from jax.sharding import PartitionSpec as P

NSTEPS = 48
STENCIL_WEIGHTS = (-205.0 / 72.0, 8.0 / 5.0, -1.0 / 5.0, 8.0 / 315.0, -1.0 / 560.0)
COURANT_SQUARED = 0.08
VELOCITY_GAIN = 0.2
PULSE_FREQUENCY = 0.05
PULSE_AMPLITUDE = 20.0

F32 = jnp.float32
BF16 = jnp.bfloat16
ROW = (((1,), (0,)), ((), ()))
TRANSPOSED_RIGHT = (((1,), (1,)), ((), ()))
TRANSPOSED_LEFT = (((0,), (0,)), ((), ()))


def hartley(length):
    index = np.arange(length)
    angle = (index[:, None] * index[None, :] % length) * (2.0 * np.pi / length)
    return np.cos(angle) + np.sin(angle)


def halves(matrix):
    high = matrix.astype(np.float32).astype(jnp.bfloat16)
    low = (matrix - high.astype(np.float64)).astype(np.float32).astype(jnp.bfloat16)
    return np.stack([high, low])


def wave_terms(length):
    return (length / 8.0) ** 2 * 4.0 * np.sin(np.arange(length) * (np.pi / length)) ** 2


def band(length):
    matrix = np.zeros((length, length))
    for offset in range(5):
        weight = STENCIL_WEIGHTS[offset] * (3.0 if offset == 0 else 1.0)
        matrix += weight * np.eye(length, k=offset)
        if offset:
            matrix += weight * np.eye(length, k=-offset)
    return matrix


def split(value):
    high = value.astype(BF16)
    return high, (value - high.astype(F32)).astype(BF16)


def dot(left, right, dims=ROW):
    return lax.dot_general(left, right, dims, preferred_element_type=F32)


def dot_3(left, right, dims=ROW):
    total = dot(left[0], right[1], dims) + dot(left[1], right[0], dims)
    return total + dot(left[0], right[0], dims)


def edges_kernel(
    sources_from, receivers_from, mean_from, logs_from, noise_from, adjoint_from, wave_from,
    xlow, xhigh, ylow, yhigh, field, speed, tilt, adjoint, sample, codes,
    mean, logs, noise, sources, receivers, sems,
):
    nx, ny, nz = speed.shape
    n_sources, n_receivers = sources.shape[1], receivers.shape[1]
    rows = [slice(0, 4), slice(nx - 4, nx), slice(4, nx - 4)]
    pairs = (
        (mean_from, mean),
        (logs_from, logs),
        (noise_from, noise),
        (adjoint_from, adjoint),
        (wave_from, field.at[0, :, 8 : ny + 8]),
    )
    copies = []
    for part in range(3):
        for i, (source, target) in enumerate(pairs):
            copy = pltpu.make_async_copy(
                source.at[rows[part]], target.at[rows[part]], sems.at[part, i]
            )
            copy.start()
            copies.append(copy)
    tables = [
        pltpu.make_async_copy(sources_from, sources, sems.at[0, 5]),
        pltpu.make_async_copy(receivers_from, receivers, sems.at[1, 5]),
    ]
    for copy in tables:
        copy.start()
    for kind in range(2):
        field[kind, :, 0:8] = jnp.zeros((nx, 8, nz), F32)
        field[kind, :, ny + 8 : ny + 16] = jnp.zeros((nx, 8, nz), F32)

    for part in range(3):
        for copy in copies[5 * part : 5 * part + 5]:
            copy.wait()
        for x in range(rows[part].start, rows[part].stop):
            spread_noise = jnp.exp(logs[x]) * noise[x]
            value = mean[x] + spread_noise
            sample[x] = value
            rate = COURANT_SQUARED * jnp.exp(2.0 * VELOCITY_GAIN * value)
            tilt[x] = spread_noise
            speed[x] = rate
            scaled = rate * adjoint[x]
            field[1, x, 8 : ny + 8] = scaled
            for kind in range(2):
                value = scaled if kind else field[0, x, 8 : ny + 8]
                if part == 0:
                    xlow[kind, x] = value
                elif part == 1:
                    xhigh[kind, x - nx + 4] = value
                half = slice(4 * (x % 2), 4 * (x % 2) + 4)
                ylow[kind, x // 2, half] = value[0:4]
                yhigh[kind, x // 2, half] = value[ny - 4 : ny]

    for copy in tables:
        copy.wait()

    def code(points):
        at_x = points[0:1] - lax.axis_index("gx") * nx
        at_y = points[1:2] - lax.axis_index("gy") * ny
        inside = (at_x >= 0) & (at_x < nx) & (at_y >= 0) & (at_y < ny)
        return jnp.where(inside, (at_x * ny + at_y) * nz + points[2:3], -1)

    codes[:, 0:n_receivers] = code(receivers)
    codes[:, n_receivers : n_receivers + n_sources] = code(sources)


def local_kernel(
    codes, prior_scale, terms_z, wave_prev_from, adjoint_next_from, bands_from, matrix_y_from, matrix_x_from,
    field, speed, adjoint,
    curved, base_wave, base_adjoint, matrix_y, matrix_x, listed, counts, gains,
    plane, wave_prev, adjoint_next, bands, sems,
):
    nx, ny, nz = speed.shape
    n_receivers = counts.shape[0] - 2
    n_sources = listed.shape[0] - 2 - n_receivers
    copies = [
        pltpu.make_async_copy(bands_from, bands, sems.at[0]),
        pltpu.make_async_copy(wave_prev_from, wave_prev, sems.at[1]),
        pltpu.make_async_copy(adjoint_next_from, adjoint_next, sems.at[2]),
        pltpu.make_async_copy(matrix_y_from, matrix_y, sems.at[3]),
        pltpu.make_async_copy(matrix_x_from, matrix_x, sems.at[4]),
    ]
    for copy in copies:
        copy.start()

    def scan(first, number, at, count):
        for i in range(number):
            listed[at + count] = first + i
            count = count + (codes[0, first + i] >= 0).astype(jnp.int32)
        return count

    copies[0].wait()
    pair = (bands[0], bands[1])
    for kind in range(2):
        for x in range(0, nx, 4):
            value = field[kind, x : x + 4, 8 : ny + 8].reshape(4 * ny, nz)
            plane[kind, x : x + 4] = dot_3(split(value), pair).reshape(4, ny, nz)
    for copy in copies[1:3]:
        copy.wait()

    def strip(t, count):
        start = pl.multiple_of(8 * t, 8)
        here = pl.ds(start, 8)
        for kind in range(2):
            centre = [field[kind, x, pl.ds(start + 8, 8)] for x in range(nx)]
            for x in range(nx):
                total = plane[kind, x, here]
                for offset in range(1, 5):
                    near_by = field[kind, x, pl.ds(start + 8 + offset, 8)]
                    near_by = near_by + field[kind, x, pl.ds(start + 8 - offset, 8)]
                    if x + offset < nx:
                        near_by = near_by + centre[x + offset]
                    if x - offset >= 0:
                        near_by = near_by + centre[x - offset]
                    total = total + STENCIL_WEIGHTS[offset] * near_by
                if kind == 0:
                    curved[x, here] = total
                    rest = 2.0 * centre[x] - wave_prev[x, here]
                    base_wave[x, here] = rest + speed[x, here] * total
                else:
                    rest = 2.0 * adjoint[x, here] - adjoint_next[x, here]
                    base_adjoint[x, here] = rest + total
        step = n_receivers // (ny // 8)
        some = scan(t * step, step, n_sources + 1, count[0])
        step = n_sources // (ny // 8)
        return some, scan(n_receivers + t * step, step, 0, count[1])

    found = lax.fori_loop(0, ny // 8, strip, (jnp.int32(0), jnp.int32(0)))
    counts[0], counts[1] = found[1], found[0]
    depth = lax.axis_index("gx") * lax.axis_size("gy") + lax.axis_index("gy")
    cells = matrix_x.shape[1] * matrix_y.shape[1] * nz
    gains[0] = prior_scale[0] * (math.sqrt(cells) / 8.0 / cells)
    gains[1] = 1.0 + terms_z[depth]
    for copy in copies[3:]:
        copy.wait()


def finish_kernel(
    codes, listed, counts, observed, step_index,
    curved, base_wave, base_adjoint, speed, tilt,
    xlow, xhigh, ylow, yhigh, forward_z,
    wave_to, adjoint_to, logscale_to, spectra,
    wave_next, adjoint_prev, logscale_grad, slope, sems,
):
    nx, ny, nz = curved.shape
    index_x, index_y = lax.axis_index("gx"), lax.axis_index("gy")
    n_receivers = counts.shape[0] - 2
    n_sources = listed.shape[0] - 2 - n_receivers
    row_at = lax.broadcasted_iota(jnp.int32, (8, nz), 0)
    lane_at = lax.broadcasted_iota(jnp.int32, (1, nz), 1)
    keep = [
        index_x > 0,
        index_x < lax.axis_size("gx") - 1,
        index_y > 0,
        index_y < lax.axis_size("gy") - 1,
    ]
    keep = [value.astype(F32) for value in keep]
    moment = jnp.full((1, nz), step_index[0] - NSTEPS // 2).astype(F32)
    moment = moment * (math.pi * PULSE_FREQUENCY)
    pulse = PULSE_AMPLITUDE * (1.0 - 2.0 * moment * moment) * jnp.exp(-moment * moment)

    def lateral_y(kind, x):
        start = jnp.zeros((8, nz), F32)
        end = jnp.zeros((8, nz), F32)
        low, high = ylow[kind, x // 2], yhigh[kind, x // 2]
        mine = row_at < 4 if x % 2 == 0 else row_at >= 4
        low, high = jnp.where(mine, low, 0.0), jnp.where(mine, high, 0.0)
        base = 0 if x % 2 == 0 else 4
        for offset in range(1, 5):
            start = start + STENCIL_WEIGHTS[offset] * pltpu.roll(low, (offset - 4 - base) % 8, 0)
            end = end + STENCIL_WEIGHTS[offset] * pltpu.roll(high, (8 - offset - base) % 8, 0)
        return jnp.where(row_at < 4, start, 0.0) * keep[2], jnp.where(row_at >= 4, end, 0.0) * keep[3]

    def change(kind, x):
        start, end = lateral_y(kind, x)
        total = jnp.concatenate([start, jnp.zeros((ny - 16, nz), F32), end], 0)
        side = None
        for offset in range(1, 5):
            if x - offset < 0:
                term = STENCIL_WEIGHTS[offset] * keep[0] * xlow[kind, x - offset + 4]
            elif x + offset >= nx:
                term = STENCIL_WEIGHTS[offset] * keep[1] * xhigh[kind, x + offset - nx]
            else:
                continue
            total = total + term
        return total

    for x in range(nx):
        more = change(0, x)
        bend = curved[x] + more
        rows = slice(x * ny, (x + 1) * ny)
        wave_next[rows] = base_wave[x] + speed[x] * more
        adjoint_prev[rows] = base_adjoint[x] + change(1, x)
        slope[rows] = (2.0 * VELOCITY_GAIN) * speed[x] * bend

    def place(point):
        code = codes[0, point]
        return pl.ds(code // nz, 1), lane_at == code % nz

    def shoot(i, _):
        row, hit = place(listed[i])
        wave_next[row] = wave_next[row] + jnp.where(hit, pulse, 0.0)
        return 0

    lax.fori_loop(0, counts[0], shoot, 0)

    def record(i, _):
        point = listed[n_sources + 1 + i]
        row, hit = place(point)
        misfit = wave_next[row] - observed[point]
        adjoint_prev[row] = adjoint_prev[row] + jnp.where(hit, misfit, 0.0)
        return 0

    lax.fori_loop(0, counts[1], record, 0)

    copies = [
        pltpu.make_async_copy(wave_next, wave_to, sems.at[0]),
        pltpu.make_async_copy(adjoint_prev, adjoint_to, sems.at[1]),
    ]
    for copy in copies:
        copy.start()
    matrix = (forward_z[0], forward_z[1])
    for j in range(nx // 2):
        rows = slice(2 * j * ny, 2 * (j + 1) * ny)
        grad = slope[rows] * adjoint_prev[rows]
        logscale_grad[rows] = grad * tilt[2 * j : 2 * j + 2].reshape(2 * ny, nz) - 1.0
        spectra[pl.ds(j, nz, stride=8)] = dot_3(matrix, split(grad), TRANSPOSED_RIGHT)
        copy = pltpu.make_async_copy(logscale_grad.at[rows], logscale_to.at[rows], sems.at[2 + j])
        copy.start()
        copies.append(copy)
    for copy in copies:
        copy.wait()


def filter_kernel(gains, spectra, matrix_y, matrix_x, terms_x, terms_y, result, plane):
    half = plane.shape[0] // 2
    tiles_x, tiles_y = spectra.shape[0], spectra.shape[1]
    lane = lax.broadcasted_iota(jnp.int32, (half, 128), 1)
    for m in range(tiles_y // 2):
        even = spectra[:, 2 * m].reshape(half, 128)
        odd = spectra[:, 2 * m + 1].reshape(half, 128)
        columns = slice(128 * m, 128 * (m + 1))
        plane[0:half, columns] = jnp.where(lane < 64, even, pltpu.roll(odd, 64, 1))
        plane[half:, columns] = jnp.where(lane < 64, pltpu.roll(even, 64, 1), odd)
    pair_y = (matrix_y[0], matrix_y[1])
    pair_x = (matrix_x[0], matrix_x[1])
    value = dot_3(split(plane[...]), pair_y)
    value = dot_3(pair_x, split(value))
    value = value * (gains[0] / ((gains[1] + terms_x[...]) + terms_y[...]))
    value = dot_3(pair_x, split(value), TRANSPOSED_LEFT)
    plane[...] = dot_3(split(value), pair_y)
    for m in range(tiles_y // 2):
        columns = slice(128 * m, 128 * (m + 1))
        even, odd = plane[0:half, columns], plane[half:, columns]
        first = jnp.where(lane < 64, even, pltpu.roll(odd, 64, 1))
        second = jnp.where(lane < 64, pltpu.roll(even, 64, 1), odd)
        result[:, 2 * m] = first.reshape(tiles_x, 8, 128)
        result[:, 2 * m + 1] = second.reshape(tiles_x, 8, 128)


def back_kernel(spectra, inverse_z, sample, search_to, search, sems):
    nx, ny, nz = sample.shape
    matrix = (inverse_z[0], inverse_z[1])
    copies = []
    for j in range(nx // 2):
        value = split(spectra[pl.ds(j, nz, stride=8)])
        smooth = dot_3(value, matrix, TRANSPOSED_LEFT)
        pair = slice(2 * j, 2 * j + 2)
        search[pair] = smooth.reshape(2, ny, nz) + sample[pair]
        copies.append(pltpu.make_async_copy(search.at[pair], search_to.at[pair], sems.at[j]))
        copies[-1].start()
    for copy in copies:
        copy.wait()


SMEM = pl.BlockSpec(memory_space=pltpu.SMEM)
VMEM = pl.BlockSpec(memory_space=pltpu.VMEM)
HBM = pl.BlockSpec(memory_space=pltpu.HBM)


def far(*sizes):
    return jax.ShapeDtypeStruct(sizes, F32)


def near(*sizes):
    return pltpu.VMEM(sizes, F32)


def call(kernel, scalars, stay, arrays, out_shape, out_specs, scratch, name):
    stay = [pltpu.with_memory_space_constraint(value, pltpu.HBM) for value in stay]
    arrays = [pltpu.with_memory_space_constraint(value, pltpu.VMEM) for value in arrays]
    return pl.pallas_call(
        kernel,
        out_shape=out_shape,
        in_specs=[SMEM] * len(scalars) + [HBM] * len(stay) + [VMEM] * len(arrays),
        out_specs=out_specs,
        scratch_shapes=scratch,
        compiler_params=pltpu.CompilerParams(vmem_limit_bytes=16 << 20),
        name=name,
    )(*scalars, *stay, *arrays)


def per_device(
    mean_field,
    log_scale,
    noise,
    wave_prev,
    wave_now,
    adjoint_next,
    adjoint_now,
    sources,
    receivers,
    observed,
    step_index,
    prior_scale,
):
    nx, ny, nz = wave_now.shape
    parts_x, parts_y = lax.axis_size("gx"), lax.axis_size("gy")
    total_x, total_y = nx * parts_x, ny * parts_y
    block = near(nx, ny, nz)
    flat = near(nx * ny, nz)

    sources, receivers = sources.T, receivers.T
    n_sources, n_receivers = sources.shape[1], receivers.shape[1]
    edge_x, edge_y = near(2, 4, ny, nz), near(2, nx // 2, 8, nz)
    xlow, xhigh, ylow, yhigh, field, speed, tilt, adjoint, sample, codes = call(
        edges_kernel,
        (),
        (sources, receivers, mean_field, log_scale, noise, adjoint_now, wave_now),
        (),
        (edge_x, edge_x, edge_y, edge_y, near(2, nx, ny + 16, nz), block, block, block, block)
        + (jax.ShapeDtypeStruct((1, n_sources + n_receivers), jnp.int32),),
        (VMEM,) * 10,
        [
            near(nx, ny, nz),
            near(nx, ny, nz),
            near(nx, ny, nz),
            pltpu.VMEM(sources.shape, jnp.int32),
            pltpu.VMEM(receivers.shape, jnp.int32),
            pltpu.SemaphoreType.DMA((3, 6)),
        ],
        "edges",
    )

    up_x = [(i, (i + 1) % parts_x) for i in range(parts_x)]
    down_x = [(j, i) for i, j in up_x]
    up_y = [(i, (i + 1) % parts_y) for i in range(parts_y)]
    down_y = [(j, i) for i, j in up_y]
    from_low_x = lax.ppermute(xhigh, "gx", up_x)
    from_high_x = lax.ppermute(xlow, "gx", down_x)
    from_low_y = lax.ppermute(yhigh, "gy", up_y)
    from_high_y = lax.ppermute(ylow, "gy", down_y)

    order = np.arange(total_x).reshape(parts_x, nx // 2, 2).transpose(2, 0, 1).reshape(-1)
    matrix_x = jnp.asarray(halves(hartley(total_x)[:, order]))
    matrix_y = jnp.asarray(halves(hartley(total_y)))
    terms_z = jnp.asarray(wave_terms(nz).astype(np.float32))
    bands = jnp.asarray(halves(band(nz)))
    curved, base_wave, base_adjoint, matrix_y, matrix_x, listed, counts, gains = call(
        local_kernel,
        (codes, prior_scale, terms_z),
        (wave_prev, adjoint_next, bands, matrix_y, matrix_x),
        (field, speed, adjoint),
        (block,) * 3
        + (
            pltpu.VMEM(matrix_y.shape, BF16),
            pltpu.VMEM(matrix_x.shape, BF16),
            jax.ShapeDtypeStruct((n_sources + n_receivers + 2,), jnp.int32),
            jax.ShapeDtypeStruct((n_receivers + 2,), jnp.int32),
            far(2),
        ),
        (VMEM,) * 5 + (SMEM,) * 3,
        [
            near(2, nx, ny, nz),
            near(nx, ny, nz),
            near(nx, ny, nz),
            pltpu.VMEM(bands.shape, BF16),
            pltpu.SemaphoreType.DMA((5,)),
        ],
        "local",
    )

    matrix_z = jnp.asarray(halves(hartley(nz)))
    wave_next, adjoint_prev, logscale_grad, spectra = call(
        finish_kernel,
        (codes, listed, counts, observed, step_index),
        (),
        (
            curved, base_wave, base_adjoint, speed, tilt,
            from_low_x, from_high_x, from_low_y, from_high_y, matrix_z,
        ),
        (pltpu.HBM((nx * ny, nz), F32),) * 3 + (far(nx * ny, nz),),
        (HBM,) * 3 + (VMEM,),
        [flat] * 4 + [pltpu.SemaphoreType.DMA((2 + nx // 2,))],
        "finish",
    )

    spectra = lax.all_to_all(
        spectra.reshape(nz, 8, nz), ("gx", "gy"), split_axis=0, concat_axis=0, tiled=True
    )

    terms_x = jnp.asarray(wave_terms(total_x).astype(np.float32)[:, None])
    terms_y = jnp.asarray(wave_terms(total_y).astype(np.float32)[None, :])
    filtered = call(
        filter_kernel,
        (gains,),
        (),
        (spectra.reshape(parts_x, parts_y, 8, nz), matrix_y, matrix_x, terms_x, terms_y),
        far(parts_x, parts_y, 8, nz),
        VMEM,
        [near(total_x, total_y)],
        "filter",
    )

    filtered = lax.all_to_all(
        filtered.reshape(nz, 8, nz), ("gx", "gy"), split_axis=0, concat_axis=0, tiled=True
    )
    search = call(
        back_kernel,
        (),
        (),
        (filtered.reshape(nx * ny, nz), matrix_z, sample),
        pltpu.HBM((nx, ny, nz), F32),
        HBM,
        [block, pltpu.SemaphoreType.DMA((nx // 2,))],
        "back",
    )
    return (
        wave_next.reshape(nx, ny, nz),
        adjoint_prev.reshape(nx, ny, nz),
        search,
        logscale_grad.reshape(nx, ny, nz),
    )


def solution(mesh):
    grid = P("gx", "gy", None)
    return jax.shard_map(
        per_device,
        mesh=mesh,
        in_specs=(grid,) * 7 + (P(),) * 5,
        out_specs=(grid,) * 4,
        check_vma=False,
    )
```

time: 64.4 us -> 64 us (level)
  blocking collectives: 17.7 us -> 41.9 us
  starting transfers between devices: 17.7 us -> 7.83 us
  waiting for transfers between devices: 9.75 us -> 0.01 us
  Pallas kernels: 15.2 us -> 12 us
  local copies, waits for them, and re-layouts: 1.58 us -> 0.03 us
    all_to_all x0 -> x1, blocking collectives: none -> 24.1 us  [per_device(): lax.all_to_all(spectra.reshape(nz, 8, nz), ('gx', 'gy'), split_axis=0, co...]
    all_to_all x1 -> x0, starting transfers between devices: 9.89 us -> none  [per_device(): lax.all_to_all(spectra.reshape(nz, 8, nz), ('gx', 'gy'), split_axis=0, co...]
    all_to_all x1 -> x0, waiting for transfers between devices: 9.74 us -> none  [per_device(): lax.all_to_all(spectra.reshape(nz, 8, nz), ('gx', 'gy'), split_axis=0, co...]
    pallas_call x6 -> x5, Pallas kernels: 15.2 us -> 12 us  [call(): pl.pallas_call(kernel, out_shape=out_shape, in_specs=[SMEM] * len(scalars...]
    unnamed x18 -> x10, local copies, waits for them, and re-layouts: 1.58 us -> 0.03 us
  transfers between devices with their start and end apart: 5 -> 4, of which waited for: 1 -> 0; matrix products, arithmetic and copies ran while one was open for 0% -> 0% of each run, Pallas kernels for 12% -> 6%
where the time goes in v2:
time: 64 us; the launch traced here: 63.8 us
  blocking collectives  41.9 us (65%)
  Pallas kernels  12 us (19%)
  starting transfers between devices  7.83 us (12%)
  between operations  2.06 us (3%)
    all_to_all x1, blocking collectives, per_device(): lax.all_to_all(spectra.reshape(nz, 8, nz), ('gx', 'gy'), split_axis=0, co...  24.1 us
    all_to_all x1, blocking collectives, per_device(): lax.all_to_all(filtered.reshape(nz, 8, nz), ('gx', 'gy'), split_axis=0, c...  17.7 us
    pallas_call x5, Pallas kernels, call(): pl.pallas_call(kernel, out_shape=out_shape, in_specs=[SMEM] * len(scalars...  12 us
    ppermute x1, starting transfers between devices, per_device(): from_low_x = lax.ppermute(xhigh, 'gx', up_x)  2.74 us
    ppermute x1, starting transfers between devices, per_device(): from_low_y = lax.ppermute(yhigh, 'gy', up_y)  2.62 us
    ppermute x1, starting transfers between devices, per_device(): from_high_y = lax.ppermute(ylow, 'gy', down_y)  2.46 us
  transfers between devices with their start and end apart: 4, of which 0 were waited for; matrix products, arithmetic and copies ran while one was open for 0% of the time, Pallas kernels for 6%

profile of v2, /device:TPU:1, one launch (start us, length us, event | category | flops | bytes accessed | tf_op | source)
XLA Modules:
  0.0 63.8 jit_solution(5235516547786255050)
XLA Ops:
  0.6 0.0 copy-start.4
  0.6 2.0 %edges.1 = (f32[2,4,64,128]{3,2,1,0:T(8,128)S(1)}, f32[2,4,64,128]{3,2,1,0:T(8,128)S(1)}, f32[2,8,8,128]{3,2,1,0:T(8,128)S(1)}, f32[2,8,8,128]{3,2,1,0:T(8,128)S...) custom-call(s32[3,16]{1,0:T(4,128)} %bitcast.14, ...), custom_call_target="tpu_custom_call" | custom-call | tf_op jit(solution)/shard_map/edges/pallas_call | solution.py:359
  2.7 2.7 %collective-permute-start = (f32[2,4,64,128]{3,2,1,0:T(8,128)S(1)}, f32[2,4,64,128]{3,2,1,0:T(8,128)S(1)}, u32[]{:S(2)}, u32[]{:S(2)}) collective-permute-start(f32[2,4,64,128]{3,2,1,0:T(8,128)S(1)} %get-tuple-element.36), channel_id=1, source_target_pairs={{0,8},{8,16},{16,24},{24,32},{32,40},{40,48},{48,56},{56,64},{64,7... | collective-permute-start | bytes 786440 | tf_op jit(solution)/shard_map/ppermute | solution.py:416
  5.4 0.0 collective-permute-start.1
  5.5 2.6 %collective-permute-start.2 = (f32[2,8,8,128]{3,2,1,0:T(8,128)S(1)}, f32[2,8,8,128]{3,2,1,0:T(8,128)S(1)}, u32[]{:S(2)}, u32[]{:S(2)}) collective-permute-start(f32[2,8,8,128]{3,2,1,0:T(8,128)S(1)} %get-tuple-element.38), channel_id=1, source_target_pairs={{0,1},{1,2},{2,3},{3,4},{4,5},{5,6},{6,7},{7,0},{8,9},{9,10},{10,1... | collective-permute-start | bytes 196616 | tf_op jit(solution)/shard_map/ppermute | solution.py:418
  8.1 2.5 %collective-permute-start.3 = (f32[2,8,8,128]{3,2,1,0:T(8,128)S(1)}, f32[2,8,8,128]{3,2,1,0:T(8,128)S(1)}, u32[]{:S(2)}, u32[]{:S(2)}) collective-permute-start(f32[2,8,8,128]{3,2,1,0:T(8,128)S(1)} %get-tuple-element.39), channel_id=1, source_target_pairs={{1,0},{2,1},{3,2},{4,3},{5,4},{6,5},{7,6},{0,7},{9,8},{10,9},{11,1... | collective-permute-start | bytes 196616 | tf_op jit(solution)/shard_map/ppermute | solution.py:419
  11.8 0.0 copy-done.4
  11.8 0.0 copy-start
  11.9 0.0 copy-start.3
  11.9 3.9 %local.1 = (f32[16,64,128]{2,1,0:T(8,128)S(1)}, f32[16,64,128]{2,1,0:T(8,128)S(1)}, f32[16,64,128]{2,1,0:T(8,128)S(1)}, bf16[2,512,512]{2,1,0:T(8,128)(2,1)S(1)}...) custom-call(s32[1,272]{1,0:T(1,128)S(1)} %get-tuple-element.26.codes, ...), custom_call_target="tpu_custom_call" | custom-call | tf_op jit(solution)/shard_map/local/pallas_call | solution.py:359
  15.7 0.0 collective-permute-done.2.ylow
  15.7 0.0 collective-permute-done.3.yhigh
  15.7 0.0 collective-permute-done.xlow
  15.8 0.0 collective-permute-done.1.xhigh
  15.8 0.0 copy-done
  15.8 0.0 copy-done.3
  15.8 0.0 copy-start.1
  15.8 0.0 copy-start.2
  15.8 2.5 %finish.1 = (f32[1024,128]{1,0:T(8,128)}, f32[1024,128]{1,0:T(8,128)}, f32[1024,128]{1,0:T(8,128)}, f32[1024,128]{1,0:T(8,128)S(1)}) custom-call(s32[1,272]{1,0:T(1,128)S(1)} %get-tuple-element.26.codes, s32[274]{0:T(512)S(1)} %get-tuple-element.30.listed, s32[258]{0:T(512)S(1)} %get-tuple-element.31.counts, f32[256]{0:T(256)S(1)} %copy-done.3, ...), custom_call_target="tpu_custom_call" | custom-call | tf_op jit(solution)/shard_map/finish/pallas_call | solution.py:359
  18.3 24.1 %all_to_all.10 = f32[128,8,128]{2,1,0:T(8,128)S(1)} all-to-all(f32[128,8,128]{2,1,0:T(8,128)S(1)} %bitcast.12), channel_id=1, replica_groups=mesh['gx'=16,'gy'=8] {'gx','gy'}, dimensions={0} | all-to-all | bytes 1048576 | tf_op jit(solution)/shard_map/all_to_all | solution.py:465
  42.4 0.0 copy-done.1
  42.4 0.0 copy-done.2
  42.4 2.5 %filter.1 = f32[16,8,8,128]{3,2,1,0:T(8,128)S(1)} custom-call(f32[2]{0:T(128)S(1)} %get-tuple-element.42.gains, f32[16,8,8,128]{3,2,1,0:T(8,128)S(1)} %bitcast.10, bf16[2,512,512]{2,1,0:T(8,128)(2,1)S(1)} %get-tuple-element.44.matrix_y, bf16[2,256,256]{2,1,0:T(8,128)(2,1)S(1)} %get-tuple-element.45.matrix_x, f32[256,1]{1,0:T(8,128)S(1)} %copy-done.1, ...), custom_call_target="tpu_custom_call" | custom-call | tf_op jit(solution)/shard_map/filter/pallas_call | solution.py:359
  44.9 17.7 %all_to_all.11 = f32[128,8,128]{2,1,0:T(8,128)S(1)} all-to-all(f32[128,8,128]{2,1,0:T(8,128)S(1)} %bitcast.11), channel_id=1, replica_groups=mesh['gx'=16,'gy'=8] {'gx','gy'}, dimensions={0} | all-to-all | bytes 1048576 | tf_op jit(solution)/shard_map/all_to_all | solution.py:482
  62.7 1.1 %back.1 = f32[16,64,128]{2,1,0:T(8,128)} custom-call(f32[1024,128]{1,0:T(8,128)S(1)} %bitcast.9, bf16[2,128,128]{2,1,0:T(8,128)(2,1)S(1)} %copy-done, f32[16,64,128]{2,1,0:T(8,128)S(1)} %get-tuple-element.46.sample), custom_call_target="tpu_custom_call" | custom-call | tf_op jit(solution)/shard_map/back/pallas_call | solution.py:359
Async XLA Ops:
  0.6 11.2 %copy-start.4 = (f32[128]{0:T(128)S(1)}, f32[128]{0:T(128)}, u32[]{:S(2)}) copy-start(f32[128]{0:T(128)} %constant.16.clone.terms_z) | copy-start | bytes 1540
  2.7 13.0 %collective-permute-start = (f32[2,4,64,128]{3,2,1,0:T(8,128)S(1)}, f32[2,4,64,128]{3,2,1,0:T(8,128)S(1)}, u32[]{:S(2)}, u32[]{:S(2)}) collective-permute-start(f32[2,4,64,128]{3,2,1,0:T(8,128)S(1)} %get-tuple-element.36), channel_id=1, source_target_pairs={{0,8},{8,16},{16,24},{24,32},{32,40},{40,48},{48,56},{56,64},{64,7... | collective-permute-start | bytes 786440 | tf_op jit(solution)/shard_map/ppermute | solution.py:416
  5.4 10.3 %collective-permute-start.1 = (f32[2,4,64,128]{3,2,1,0:T(8,128)S(1)}, f32[2,4,64,128]{3,2,1,0:T(8,128)S(1)}, u32[]{:S(2)}, u32[]{:S(2)}) collective-permute-start(f32[2,4,64,128]{3,2,1,0:T(8,128)S(1)} %get-tuple-element.37), channel_id=1, source_target_pairs={{8,0},{16,8},{24,16},{32,24},{40,32},{48,40},{56,48},{64,56},{72,6... | collective-permute-start | bytes 786440 | tf_op jit(solution)/shard_map/ppermute | solution.py:417
  5.5 10.3 %collective-permute-start.2 = (f32[2,8,8,128]{3,2,1,0:T(8,128)S(1)}, f32[2,8,8,128]{3,2,1,0:T(8,128)S(1)}, u32[]{:S(2)}, u32[]{:S(2)}) collective-permute-start(f32[2,8,8,128]{3,2,1,0:T(8,128)S(1)} %get-tuple-element.38), channel_id=1, source_target_pairs={{0,1},{1,2},{2,3},{3,4},{4,5},{5,6},{6,7},{7,0},{8,9},{9,10},{10,1... | collective-permute-start | bytes 196616 | tf_op jit(solution)/shard_map/ppermute | solution.py:418
  8.1 7.7 %collective-permute-start.3 = (f32[2,8,8,128]{3,2,1,0:T(8,128)S(1)}, f32[2,8,8,128]{3,2,1,0:T(8,128)S(1)}, u32[]{:S(2)}, u32[]{:S(2)}) collective-permute-start(f32[2,8,8,128]{3,2,1,0:T(8,128)S(1)} %get-tuple-element.39), channel_id=1, source_target_pairs={{1,0},{2,1},{3,2},{4,3},{5,4},{6,5},{7,6},{0,7},{9,8},{10,9},{11,1... | collective-permute-start | bytes 196616 | tf_op jit(solution)/shard_map/ppermute | solution.py:419
  11.8 3.9 %copy-start = (bf16[2,128,128]{2,1,0:T(8,128)(2,1)S(1)}, bf16[2,128,128]{2,1,0:T(8,128)(2,1)}, u32[]{:S(2)}) copy-start(bf16[2,128,128]{2,1,0:T(8,128)(2,1)} %constant.18.clone.forward_z.inverse_z) | copy-start | bytes 196612
  11.9 3.9 %copy-start.3 = (f32[256]{0:T(256)S(1)}, f32[256]{0:T(256)}, u32[]{:S(2)}) copy-start(f32[256]{0:T(256)} %observed.1) | copy-start | bytes 3076
  15.8 26.6 %copy-start.1 = (f32[256,1]{1,0:T(8,128)S(1)}, f32[256,1]{1,0:T(8,128)}, u32[]{:S(2)}) copy-start(f32[256,1]{1,0:T(8,128)} %constant.19.clone.terms_x) | copy-start | bytes 3076
  15.8 26.6 %copy-start.2 = (f32[1,512]{1,0:T(1,128)S(1)}, f32[1,512]{1,0:T(1,128)}, u32[]{:S(2)}) copy-start(f32[1,512]{1,0:T(1,128)} %constant.20.clone.terms_y) | copy-start | bytes 6148

commit v3 on v2

--- a/solution.py
+++ b/solution.py
@@ -59,8 +59,14 @@
 
 
 def dot_3(left, right, dims=ROW):
-    total = dot(left[0], right[1], dims) + dot(left[1], right[0], dims)
-    return total + dot(left[0], right[0], dims)
+    (on_left,), (on_right,) = dims[0]
+    if left[0].shape[on_left] <= 128:
+        cross = dot(
+            jnp.concatenate(left, axis=on_left), jnp.concatenate(right[::-1], axis=on_right), dims
+        )
+    else:
+        cross = dot(left[0], right[1], dims) + dot(left[1], right[0], dims)
+    return cross + dot(left[0], right[0], dims)
 
 
 def edges_kernel(
@@ -238,27 +244,36 @@
             end = end + STENCIL_WEIGHTS[offset] * pltpu.roll(high, (8 - offset - base) % 8, 0)
         return jnp.where(row_at < 4, start, 0.0) * keep[2], jnp.where(row_at >= 4, end, 0.0) * keep[3]
 
-    def change(kind, x):
-        start, end = lateral_y(kind, x)
-        total = jnp.concatenate([start, jnp.zeros((ny - 16, nz), F32), end], 0)
-        side = None
+    def change(kind, x, edges, first, last):
+        total = None
+        if first == 0:
+            total = edges[0]
+        elif last == ny:
+            total = edges[1]
         for offset in range(1, 5):
             if x - offset < 0:
-                term = STENCIL_WEIGHTS[offset] * keep[0] * xlow[kind, x - offset + 4]
+                layer, weight = xlow[kind, x - offset + 4, first:last], keep[0]
             elif x + offset >= nx:
-                term = STENCIL_WEIGHTS[offset] * keep[1] * xhigh[kind, x + offset - nx]
+                layer, weight = xhigh[kind, x + offset - nx, first:last], keep[1]
             else:
                 continue
-            total = total + term
+            term = STENCIL_WEIGHTS[offset] * weight * layer
+            total = term if total is None else total + term
         return total
 
     for x in range(nx):
-        more = change(0, x)
-        bend = curved[x] + more
-        rows = slice(x * ny, (x + 1) * ny)
-        wave_next[rows] = base_wave[x] + speed[x] * more
-        adjoint_prev[rows] = base_adjoint[x] + change(1, x)
-        slope[rows] = (2.0 * VELOCITY_GAIN) * speed[x] * bend
+        edges = [lateral_y(kind, x) for kind in range(2)]
+        for first, last in ((0, 8), (8, ny - 8), (ny - 8, ny)):
+            rows = slice(x * ny + first, x * ny + last)
+            bend, rate = curved[x, first:last], speed[x, first:last]
+            onward, backward = base_wave[x, first:last], base_adjoint[x, first:last]
+            more = change(0, x, edges[0], first, last)
+            if more is not None:
+                bend, onward = bend + more, onward + rate * more
+                backward = backward + change(1, x, edges[1], first, last)
+            wave_next[rows] = onward
+            adjoint_prev[rows] = backward
+            slope[rows] = (2.0 * VELOCITY_GAIN) * rate * bend
 
     def place(point):
         code = codes[0, point]

time: 64 us -> 63.8 us (level)
  no operation moved by 1% of the time
where the time goes in v3:
time: 63.8 us; the launch traced here: 63.6 us
  blocking collectives  41.9 us (66%)
  Pallas kernels  11.8 us (18%)
  starting transfers between devices  7.83 us (12%)
  between operations  2.06 us (3%)
    all_to_all x1, blocking collectives, per_device(): lax.all_to_all(spectra.reshape(nz, 8, nz), ('gx', 'gy'), split_axis=0, co...  24.1 us
    all_to_all x1, blocking collectives, per_device(): lax.all_to_all(filtered.reshape(nz, 8, nz), ('gx', 'gy'), split_axis=0, c...  17.8 us
    pallas_call x5, Pallas kernels, call(): pl.pallas_call(kernel, out_shape=out_shape, in_specs=[SMEM] * len(scalars...  11.8 us
    ppermute x1, starting transfers between devices, per_device(): from_low_x = lax.ppermute(xhigh, 'gx', up_x)  2.74 us
    ppermute x1, starting transfers between devices, per_device(): from_low_y = lax.ppermute(yhigh, 'gy', up_y)  2.62 us
    ppermute x1, starting transfers between devices, per_device(): from_high_y = lax.ppermute(ylow, 'gy', down_y)  2.46 us
  transfers between devices with their start and end apart: 4, of which 0 were waited for; matrix products, arithmetic and copies ran while one was open for 0% of the time, Pallas kernels for 6%

profile of v3, /device:TPU:1, one launch (start us, length us, event | category | flops | bytes accessed | tf_op | source)
XLA Modules:
  0.0 63.6 jit_solution(6269978238593450345)
XLA Ops:
  0.6 0.0 copy-start.4
  0.6 2.0 %edges.1 = (f32[2,4,64,128]{3,2,1,0:T(8,128)S(1)}, f32[2,4,64,128]{3,2,1,0:T(8,128)S(1)}, f32[2,8,8,128]{3,2,1,0:T(8,128)S(1)}, f32[2,8,8,128]{3,2,1,0:T(8,128)S...) custom-call(s32[3,16]{1,0:T(4,128)} %bitcast.14, ...), custom_call_target="tpu_custom_call" | custom-call | tf_op jit(solution)/shard_map/edges/pallas_call | solution.py:374
  2.7 2.7 %collective-permute-start = (f32[2,4,64,128]{3,2,1,0:T(8,128)S(1)}, f32[2,4,64,128]{3,2,1,0:T(8,128)S(1)}, u32[]{:S(2)}, u32[]{:S(2)}) collective-permute-start(f32[2,4,64,128]{3,2,1,0:T(8,128)S(1)} %get-tuple-element.36), channel_id=1, source_target_pairs={{0,8},{8,16},{16,24},{24,32},{32,40},{40,48},{48,56},{56,64},{64,7... | collective-permute-start | bytes 786440 | tf_op jit(solution)/shard_map/ppermute | solution.py:431
  5.4 0.0 collective-permute-start.1
  5.5 2.6 %collective-permute-start.2 = (f32[2,8,8,128]{3,2,1,0:T(8,128)S(1)}, f32[2,8,8,128]{3,2,1,0:T(8,128)S(1)}, u32[]{:S(2)}, u32[]{:S(2)}) collective-permute-start(f32[2,8,8,128]{3,2,1,0:T(8,128)S(1)} %get-tuple-element.38), channel_id=1, source_target_pairs={{0,1},{1,2},{2,3},{3,4},{4,5},{5,6},{6,7},{7,0},{8,9},{9,10},{10,1... | collective-permute-start | bytes 196616 | tf_op jit(solution)/shard_map/ppermute | solution.py:433
  8.1 2.5 %collective-permute-start.3 = (f32[2,8,8,128]{3,2,1,0:T(8,128)S(1)}, f32[2,8,8,128]{3,2,1,0:T(8,128)S(1)}, u32[]{:S(2)}, u32[]{:S(2)}) collective-permute-start(f32[2,8,8,128]{3,2,1,0:T(8,128)S(1)} %get-tuple-element.39), channel_id=1, source_target_pairs={{1,0},{2,1},{3,2},{4,3},{5,4},{6,5},{7,6},{0,7},{9,8},{10,9},{11,1... | collective-permute-start | bytes 196616 | tf_op jit(solution)/shard_map/ppermute | solution.py:434
  11.8 0.0 copy-done.4
  11.8 0.0 copy-start
  11.9 0.0 copy-start.3
  11.9 3.9 %local.1 = (f32[16,64,128]{2,1,0:T(8,128)S(1)}, f32[16,64,128]{2,1,0:T(8,128)S(1)}, f32[16,64,128]{2,1,0:T(8,128)S(1)}, bf16[2,512,512]{2,1,0:T(8,128)(2,1)S(1)}...) custom-call(s32[1,272]{1,0:T(1,128)S(1)} %get-tuple-element.26.codes, ...), custom_call_target="tpu_custom_call" | custom-call | tf_op jit(solution)/shard_map/local/pallas_call | solution.py:374
  15.7 0.0 collective-permute-done.2.ylow
  15.7 0.0 collective-permute-done.3.yhigh
  15.7 0.0 collective-permute-done.xlow
  15.8 0.0 collective-permute-done.1.xhigh
  15.8 0.0 copy-done
  15.8 0.0 copy-done.3
  15.8 0.0 copy-start.1
  15.8 0.0 copy-start.2
  15.8 2.3 %finish.1 = (f32[1024,128]{1,0:T(8,128)}, f32[1024,128]{1,0:T(8,128)}, f32[1024,128]{1,0:T(8,128)}, f32[1024,128]{1,0:T(8,128)S(1)}) custom-call(s32[1,272]{1,0:T(1,128)S(1)} %get-tuple-element.26.codes, s32[274]{0:T(512)S(1)} %get-tuple-element.30.listed, s32[258]{0:T(512)S(1)} %get-tuple-element.31.counts, f32[256]{0:T(256)S(1)} %copy-done.3, ...), custom_call_target="tpu_custom_call" | custom-call | tf_op jit(solution)/shard_map/finish/pallas_call | solution.py:374
  18.1 24.1 %all_to_all.10 = f32[128,8,128]{2,1,0:T(8,128)S(1)} all-to-all(f32[128,8,128]{2,1,0:T(8,128)S(1)} %bitcast.12), channel_id=1, replica_groups=mesh['gx'=16,'gy'=8] {'gx','gy'}, dimensions={0} | all-to-all | bytes 1048576 | tf_op jit(solution)/shard_map/all_to_all | solution.py:480
  42.2 0.0 copy-done.1
  42.2 0.0 copy-done.2
  42.2 2.5 %filter.1 = f32[16,8,8,128]{3,2,1,0:T(8,128)S(1)} custom-call(f32[2]{0:T(128)S(1)} %get-tuple-element.42.gains, f32[16,8,8,128]{3,2,1,0:T(8,128)S(1)} %bitcast.10, bf16[2,512,512]{2,1,0:T(8,128)(2,1)S(1)} %get-tuple-element.44.matrix_y, bf16[2,256,256]{2,1,0:T(8,128)(2,1)S(1)} %get-tuple-element.45.matrix_x, f32[256,1]{1,0:T(8,128)S(1)} %copy-done.1, ...), custom_call_target="tpu_custom_call" | custom-call | tf_op jit(solution)/shard_map/filter/pallas_call | solution.py:374
  44.7 17.8 %all_to_all.11 = f32[128,8,128]{2,1,0:T(8,128)S(1)} all-to-all(f32[128,8,128]{2,1,0:T(8,128)S(1)} %bitcast.11), channel_id=1, replica_groups=mesh['gx'=16,'gy'=8] {'gx','gy'}, dimensions={0} | all-to-all | bytes 1048576 | tf_op jit(solution)/shard_map/all_to_all | solution.py:497
  62.5 1.1 %back.1 = f32[16,64,128]{2,1,0:T(8,128)} custom-call(f32[1024,128]{1,0:T(8,128)S(1)} %bitcast.9, bf16[2,128,128]{2,1,0:T(8,128)(2,1)S(1)} %copy-done, f32[16,64,128]{2,1,0:T(8,128)S(1)} %get-tuple-element.46.sample), custom_call_target="tpu_custom_call" | custom-call | tf_op jit(solution)/shard_map/back/pallas_call | solution.py:374
Async XLA Ops:
  0.6 11.2 %copy-start.4 = (f32[128]{0:T(128)S(1)}, f32[128]{0:T(128)}, u32[]{:S(2)}) copy-start(f32[128]{0:T(128)} %constant.16.clone.terms_z) | copy-start | bytes 1540
  2.7 13.0 %collective-permute-start = (f32[2,4,64,128]{3,2,1,0:T(8,128)S(1)}, f32[2,4,64,128]{3,2,1,0:T(8,128)S(1)}, u32[]{:S(2)}, u32[]{:S(2)}) collective-permute-start(f32[2,4,64,128]{3,2,1,0:T(8,128)S(1)} %get-tuple-element.36), channel_id=1, source_target_pairs={{0,8},{8,16},{16,24},{24,32},{32,40},{40,48},{48,56},{56,64},{64,7... | collective-permute-start | bytes 786440 | tf_op jit(solution)/shard_map/ppermute | solution.py:431
  5.4 10.3 %collective-permute-start.1 = (f32[2,4,64,128]{3,2,1,0:T(8,128)S(1)}, f32[2,4,64,128]{3,2,1,0:T(8,128)S(1)}, u32[]{:S(2)}, u32[]{:S(2)}) collective-permute-start(f32[2,4,64,128]{3,2,1,0:T(8,128)S(1)} %get-tuple-element.37), channel_id=1, source_target_pairs={{8,0},{16,8},{24,16},{32,24},{40,32},{48,40},{56,48},{64,56},{72,6... | collective-permute-start | bytes 786440 | tf_op jit(solution)/shard_map/ppermute | solution.py:432
  5.5 10.3 %collective-permute-start.2 = (f32[2,8,8,128]{3,2,1,0:T(8,128)S(1)}, f32[2,8,8,128]{3,2,1,0:T(8,128)S(1)}, u32[]{:S(2)}, u32[]{:S(2)}) collective-permute-start(f32[2,8,8,128]{3,2,1,0:T(8,128)S(1)} %get-tuple-element.38), channel_id=1, source_target_pairs={{0,1},{1,2},{2,3},{3,4},{4,5},{5,6},{6,7},{7,0},{8,9},{9,10},{10,1... | collective-permute-start | bytes 196616 | tf_op jit(solution)/shard_map/ppermute | solution.py:433
  8.1 7.7 %collective-permute-start.3 = (f32[2,8,8,128]{3,2,1,0:T(8,128)S(1)}, f32[2,8,8,128]{3,2,1,0:T(8,128)S(1)}, u32[]{:S(2)}, u32[]{:S(2)}) collective-permute-start(f32[2,8,8,128]{3,2,1,0:T(8,128)S(1)} %get-tuple-element.39), channel_id=1, source_target_pairs={{1,0},{2,1},{3,2},{4,3},{5,4},{6,5},{7,6},{0,7},{9,8},{10,9},{11,1... | collective-permute-start | bytes 196616 | tf_op jit(solution)/shard_map/ppermute | solution.py:434
  11.8 3.9 %copy-start = (bf16[2,128,128]{2,1,0:T(8,128)(2,1)S(1)}, bf16[2,128,128]{2,1,0:T(8,128)(2,1)}, u32[]{:S(2)}) copy-start(bf16[2,128,128]{2,1,0:T(8,128)(2,1)} %constant.18.clone.forward_z.inverse_z) | copy-start | bytes 196612
  11.9 3.9 %copy-start.3 = (f32[256]{0:T(256)S(1)}, f32[256]{0:T(256)}, u32[]{:S(2)}) copy-start(f32[256]{0:T(256)} %observed.1) | copy-start | bytes 3076
  15.8 26.4 %copy-start.1 = (f32[256,1]{1,0:T(8,128)S(1)}, f32[256,1]{1,0:T(8,128)}, u32[]{:S(2)}) copy-start(f32[256,1]{1,0:T(8,128)} %constant.19.clone.terms_x) | copy-start | bytes 3076
  15.8 26.4 %copy-start.2 = (f32[1,512]{1,0:T(1,128)S(1)}, f32[1,512]{1,0:T(1,128)}, u32[]{:S(2)}) copy-start(f32[1,512]{1,0:T(1,128)} %constant.20.clone.terms_y) | copy-start | bytes 6148

commit v4 on v3

--- a/solution.py
+++ b/solution.py
@@ -76,7 +76,7 @@
 ):
     nx, ny, nz = speed.shape
     n_sources, n_receivers = sources.shape[1], receivers.shape[1]
-    rows = [slice(0, 4), slice(nx - 4, nx), slice(4, nx - 4)]
+    rows = [slice(0, 4), slice(nx - 4, nx), slice(4, nx // 2), slice(nx // 2, nx - 4)]
     pairs = (
         (mean_from, mean),
         (logs_from, logs),
@@ -85,7 +85,7 @@
         (wave_from, field.at[0, :, 8 : ny + 8]),
     )
     copies = []
-    for part in range(3):
+    for part in range(4):
         for i, (source, target) in enumerate(pairs):
             copy = pltpu.make_async_copy(
                 source.at[rows[part]], target.at[rows[part]], sems.at[part, i]
@@ -102,7 +102,7 @@
         field[kind, :, 0:8] = jnp.zeros((nx, 8, nz), F32)
         field[kind, :, ny + 8 : ny + 16] = jnp.zeros((nx, 8, nz), F32)
 
-    for part in range(3):
+    for part in range(4):
         for copy in copies[5 * part : 5 * part + 5]:
             copy.wait()
         for x in range(rows[part].start, rows[part].stop):
@@ -419,7 +419,7 @@
             near(nx, ny, nz),
             pltpu.VMEM(sources.shape, jnp.int32),
             pltpu.VMEM(receivers.shape, jnp.int32),
-            pltpu.SemaphoreType.DMA((3, 6)),
+            pltpu.SemaphoreType.DMA((4, 6)),
         ],
         "edges",
     )

time: 63.8 us -> 63.8 us (level)
  no operation moved by 1% of the time
where the time goes in v4:
time: 63.8 us; the launch traced here: 63.6 us
  blocking collectives  41.9 us (66%)
  Pallas kernels  11.8 us (18%)
  starting transfers between devices  7.83 us (12%)
  between operations  2.06 us (3%)
    all_to_all x1, blocking collectives, per_device(): lax.all_to_all(spectra.reshape(nz, 8, nz), ('gx', 'gy'), split_axis=0, co...  24.1 us
    all_to_all x1, blocking collectives, per_device(): lax.all_to_all(filtered.reshape(nz, 8, nz), ('gx', 'gy'), split_axis=0, c...  17.8 us
    pallas_call x5, Pallas kernels, call(): pl.pallas_call(kernel, out_shape=out_shape, in_specs=[SMEM] * len(scalars...  11.8 us
    ppermute x1, starting transfers between devices, per_device(): from_low_x = lax.ppermute(xhigh, 'gx', up_x)  2.74 us
    ppermute x1, starting transfers between devices, per_device(): from_low_y = lax.ppermute(yhigh, 'gy', up_y)  2.62 us
    ppermute x1, starting transfers between devices, per_device(): from_high_y = lax.ppermute(ylow, 'gy', down_y)  2.46 us
  transfers between devices with their start and end apart: 4, of which 0 were waited for; matrix products, arithmetic and copies ran while one was open for 0% of the time, Pallas kernels for 6%

profile of v4, /device:TPU:1, one launch (start us, length us, event | category | flops | bytes accessed | tf_op | source)
XLA Modules:
  0.0 63.6 jit_solution(4759472400219920349)
XLA Ops:
  0.6 0.0 copy-start.4
  0.6 2.0 %edges.1 = (f32[2,4,64,128]{3,2,1,0:T(8,128)S(1)}, f32[2,4,64,128]{3,2,1,0:T(8,128)S(1)}, f32[2,8,8,128]{3,2,1,0:T(8,128)S(1)}, f32[2,8,8,128]{3,2,1,0:T(8,128)S...) custom-call(s32[3,16]{1,0:T(4,128)} %bitcast.14, ...), custom_call_target="tpu_custom_call" | custom-call | tf_op jit(solution)/shard_map/edges/pallas_call | solution.py:374
  2.7 2.7 %collective-permute-start = (f32[2,4,64,128]{3,2,1,0:T(8,128)S(1)}, f32[2,4,64,128]{3,2,1,0:T(8,128)S(1)}, u32[]{:S(2)}, u32[]{:S(2)}) collective-permute-start(f32[2,4,64,128]{3,2,1,0:T(8,128)S(1)} %get-tuple-element.36), channel_id=1, source_target_pairs={{0,8},{8,16},{16,24},{24,32},{32,40},{40,48},{48,56},{56,64},{64,7... | collective-permute-start | bytes 786440 | tf_op jit(solution)/shard_map/ppermute | solution.py:431
  5.4 0.0 collective-permute-start.1
  5.4 2.6 %collective-permute-start.2 = (f32[2,8,8,128]{3,2,1,0:T(8,128)S(1)}, f32[2,8,8,128]{3,2,1,0:T(8,128)S(1)}, u32[]{:S(2)}, u32[]{:S(2)}) collective-permute-start(f32[2,8,8,128]{3,2,1,0:T(8,128)S(1)} %get-tuple-element.38), channel_id=1, source_target_pairs={{0,1},{1,2},{2,3},{3,4},{4,5},{5,6},{6,7},{7,0},{8,9},{9,10},{10,1... | collective-permute-start | bytes 196616 | tf_op jit(solution)/shard_map/ppermute | solution.py:433
  8.1 2.5 %collective-permute-start.3 = (f32[2,8,8,128]{3,2,1,0:T(8,128)S(1)}, f32[2,8,8,128]{3,2,1,0:T(8,128)S(1)}, u32[]{:S(2)}, u32[]{:S(2)}) collective-permute-start(f32[2,8,8,128]{3,2,1,0:T(8,128)S(1)} %get-tuple-element.39), channel_id=1, source_target_pairs={{1,0},{2,1},{3,2},{4,3},{5,4},{6,5},{7,6},{0,7},{9,8},{10,9},{11,1... | collective-permute-start | bytes 196616 | tf_op jit(solution)/shard_map/ppermute | solution.py:434
  11.8 0.0 copy-done.4
  11.8 0.0 copy-start
  11.8 0.0 copy-start.3
  11.9 3.8 %local.1 = (f32[16,64,128]{2,1,0:T(8,128)S(1)}, f32[16,64,128]{2,1,0:T(8,128)S(1)}, f32[16,64,128]{2,1,0:T(8,128)S(1)}, bf16[2,512,512]{2,1,0:T(8,128)(2,1)S(1)}...) custom-call(s32[1,272]{1,0:T(1,128)S(1)} %get-tuple-element.26.codes, ...), custom_call_target="tpu_custom_call" | custom-call | tf_op jit(solution)/shard_map/local/pallas_call | solution.py:374
  15.7 0.0 collective-permute-done.2.ylow
  15.7 0.0 collective-permute-done.3.yhigh
  15.7 0.0 collective-permute-done.xlow
  15.7 0.0 collective-permute-done.1.xhigh
  15.8 0.0 copy-done
  15.8 0.0 copy-done.3
  15.8 0.0 copy-start.1
  15.8 0.0 copy-start.2
  15.8 2.3 %finish.1 = (f32[1024,128]{1,0:T(8,128)}, f32[1024,128]{1,0:T(8,128)}, f32[1024,128]{1,0:T(8,128)}, f32[1024,128]{1,0:T(8,128)S(1)}) custom-call(s32[1,272]{1,0:T(1,128)S(1)} %get-tuple-element.26.codes, s32[274]{0:T(512)S(1)} %get-tuple-element.30.listed, s32[258]{0:T(512)S(1)} %get-tuple-element.31.counts, f32[256]{0:T(256)S(1)} %copy-done.3, ...), custom_call_target="tpu_custom_call" | custom-call | tf_op jit(solution)/shard_map/finish/pallas_call | solution.py:374
  18.1 24.1 %all_to_all.10 = f32[128,8,128]{2,1,0:T(8,128)S(1)} all-to-all(f32[128,8,128]{2,1,0:T(8,128)S(1)} %bitcast.12), channel_id=1, replica_groups=mesh['gx'=16,'gy'=8] {'gx','gy'}, dimensions={0} | all-to-all | bytes 1048576 | tf_op jit(solution)/shard_map/all_to_all | solution.py:480
  42.2 0.0 copy-done.1
  42.2 0.0 copy-done.2
  42.2 2.5 %filter.1 = f32[16,8,8,128]{3,2,1,0:T(8,128)S(1)} custom-call(f32[2]{0:T(128)S(1)} %get-tuple-element.42.gains, f32[16,8,8,128]{3,2,1,0:T(8,128)S(1)} %bitcast.10, bf16[2,512,512]{2,1,0:T(8,128)(2,1)S(1)} %get-tuple-element.44.matrix_y, bf16[2,256,256]{2,1,0:T(8,128)(2,1)S(1)} %get-tuple-element.45.matrix_x, f32[256,1]{1,0:T(8,128)S(1)} %copy-done.1, ...), custom_call_target="tpu_custom_call" | custom-call | tf_op jit(solution)/shard_map/filter/pallas_call | solution.py:374
  44.7 17.8 %all_to_all.11 = f32[128,8,128]{2,1,0:T(8,128)S(1)} all-to-all(f32[128,8,128]{2,1,0:T(8,128)S(1)} %bitcast.11), channel_id=1, replica_groups=mesh['gx'=16,'gy'=8] {'gx','gy'}, dimensions={0} | all-to-all | bytes 1048576 | tf_op jit(solution)/shard_map/all_to_all | solution.py:497
  62.5 1.1 %back.1 = f32[16,64,128]{2,1,0:T(8,128)} custom-call(f32[1024,128]{1,0:T(8,128)S(1)} %bitcast.9, bf16[2,128,128]{2,1,0:T(8,128)(2,1)S(1)} %copy-done, f32[16,64,128]{2,1,0:T(8,128)S(1)} %get-tuple-element.46.sample), custom_call_target="tpu_custom_call" | custom-call | tf_op jit(solution)/shard_map/back/pallas_call | solution.py:374
Async XLA Ops:
  0.6 11.2 %copy-start.4 = (f32[128]{0:T(128)S(1)}, f32[128]{0:T(128)}, u32[]{:S(2)}) copy-start(f32[128]{0:T(128)} %constant.16.clone.terms_z) | copy-start | bytes 1540
  2.7 13.0 %collective-permute-start = (f32[2,4,64,128]{3,2,1,0:T(8,128)S(1)}, f32[2,4,64,128]{3,2,1,0:T(8,128)S(1)}, u32[]{:S(2)}, u32[]{:S(2)}) collective-permute-start(f32[2,4,64,128]{3,2,1,0:T(8,128)S(1)} %get-tuple-element.36), channel_id=1, source_target_pairs={{0,8},{8,16},{16,24},{24,32},{32,40},{40,48},{48,56},{56,64},{64,7... | collective-permute-start | bytes 786440 | tf_op jit(solution)/shard_map/ppermute | solution.py:431
  5.4 10.3 %collective-permute-start.1 = (f32[2,4,64,128]{3,2,1,0:T(8,128)S(1)}, f32[2,4,64,128]{3,2,1,0:T(8,128)S(1)}, u32[]{:S(2)}, u32[]{:S(2)}) collective-permute-start(f32[2,4,64,128]{3,2,1,0:T(8,128)S(1)} %get-tuple-element.37), channel_id=1, source_target_pairs={{8,0},{16,8},{24,16},{32,24},{40,32},{48,40},{56,48},{64,56},{72,6... | collective-permute-start | bytes 786440 | tf_op jit(solution)/shard_map/ppermute | solution.py:432
  5.4 10.3 %collective-permute-start.2 = (f32[2,8,8,128]{3,2,1,0:T(8,128)S(1)}, f32[2,8,8,128]{3,2,1,0:T(8,128)S(1)}, u32[]{:S(2)}, u32[]{:S(2)}) collective-permute-start(f32[2,8,8,128]{3,2,1,0:T(8,128)S(1)} %get-tuple-element.38), channel_id=1, source_target_pairs={{0,1},{1,2},{2,3},{3,4},{4,5},{5,6},{6,7},{7,0},{8,9},{9,10},{10,1... | collective-permute-start | bytes 196616 | tf_op jit(solution)/shard_map/ppermute | solution.py:433
  8.1 7.7 %collective-permute-start.3 = (f32[2,8,8,128]{3,2,1,0:T(8,128)S(1)}, f32[2,8,8,128]{3,2,1,0:T(8,128)S(1)}, u32[]{:S(2)}, u32[]{:S(2)}) collective-permute-start(f32[2,8,8,128]{3,2,1,0:T(8,128)S(1)} %get-tuple-element.39), channel_id=1, source_target_pairs={{1,0},{2,1},{3,2},{4,3},{5,4},{6,5},{7,6},{0,7},{9,8},{10,9},{11,1... | collective-permute-start | bytes 196616 | tf_op jit(solution)/shard_map/ppermute | solution.py:434
  11.8 3.9 %copy-start = (bf16[2,128,128]{2,1,0:T(8,128)(2,1)S(1)}, bf16[2,128,128]{2,1,0:T(8,128)(2,1)}, u32[]{:S(2)}) copy-start(bf16[2,128,128]{2,1,0:T(8,128)(2,1)} %constant.18.clone.forward_z.inverse_z) | copy-start | bytes 196612
  11.8 3.9 %copy-start.3 = (f32[256]{0:T(256)S(1)}, f32[256]{0:T(256)}, u32[]{:S(2)}) copy-start(f32[256]{0:T(256)} %observed.1) | copy-start | bytes 3076
  15.8 26.4 %copy-start.1 = (f32[256,1]{1,0:T(8,128)S(1)}, f32[256,1]{1,0:T(8,128)}, u32[]{:S(2)}) copy-start(f32[256,1]{1,0:T(8,128)} %constant.19.clone.terms_x) | copy-start | bytes 3076
  15.8 26.4 %copy-start.2 = (f32[1,512]{1,0:T(1,128)S(1)}, f32[1,512]{1,0:T(1,128)}, u32[]{:S(2)}) copy-start(f32[1,512]{1,0:T(1,128)} %constant.20.clone.terms_y) | copy-start | bytes 6148
